TPU v7x, 32 devices: a whole 2x2x4 slice. The times are simulated.
32 devices in a mesh: region: 4 (over y, x), wave: 8 (over z, core).
Axes of the slice: x: 2, y: 2, z: 4, core: 2. Of those that a mesh axis runs over, the one named last changes fastest.
Arguments:
- state0: float32 [9, 35, 8192], P(None, None, ('region', 'wave')), may hold values from -6 to 6
- delta: float32 [9, 35, 8192], P(None, None, ('region', 'wave')), may hold values from -6 to 6
- adjoint: float32 [9, 35, 8192], P(None, None, ('region', 'wave')), may hold values from -6 to 6
- model: float32 [3, 35, 8192], P(None, None, ('region', 'wave')), may hold values from 0.5 to 2
- geometry: float32 [9, 8192], P(None, ('region', 'wave')), may hold values from -4 to 4
- normals: float32 [3, 4, 8192], P(None, None, ('region', 'wave')), may hold values from -1 to 1
- face_scale: float32 [4, 8192], P(None, ('region', 'wave')), may hold values from 0.5 to 2
- derivative: float32 [3, 35, 35], replicated, may hold values from -1 to 1
- lift: float32 [4, 35, 15], replicated, may hold values from -1.5 to 1.5
- prolong: float32 [8, 35, 10], replicated, may hold values from -2 to 2
- coarse_step: float32 [30, 1024], P(None, ('region', 'wave')), may hold values from -6 to 6
- reg_weight: float32 [30, 1024], P(None, ('region', 'wave')), may hold values from 1 to 10
- observe: float32 [35, 8192], P(None, ('region', 'wave')), may hold values from 0.1 to 1
- owner: int32 [8192, 1], P(('region', 'wave')), may hold values from 0 to 31; in each aligned block of 256 rows (0 to 255, 256 to 511, ...) at most 16 rows name the same one
- coarse_local: int32 [8192], P(('region', 'wave')), may hold values from 0 to 31
- child: int32 [8192], P(('region', 'wave')), may hold values from 0 to 7
- neighbor: int32 [4, 8192], P(None, ('region', 'wave')), may hold values from 0 to 1151
- orient: int32 [4, 8192], P(None, ('region', 'wave')), may hold values from 0 to 5
- send_face: int32 [4096], P(('region', 'wave')), may hold values from 0 to 1023
Outputs:
- delta_next: float32 [9, 35, 8192], P(None, None, ('region', 'wave'))
- adjoint_next: float32 [9, 35, 8192], P(None, None, ('region', 'wave'))
- hess_vec: float32 [30, 1024], P(None, ('region', 'wave'))
Inputs may be any that keep to these rules, and one draw needn't show every extreme that they name: `owner`: no more than 16 fine elements of one device have coarse elements owned by one device, and that number is reached. `send_face`: entries w * 16 to w * 16 + 15 of a device name its traces for wave partition w.
All inputs are finite; a program needn't handle non-finite values.
Results may differ from a plain program's by a relative error of at most 0.0003.
Values sent between devices are 32-bit elements; how exact they have to be, the bound alone decides.
No kernel may reach another device: no remote copies, remote signals or barrier semaphores. Data moves between devices by JAX's collectives and lax.ppermute only.
A program may use at most 128 MiB of HBM per device.

v0:
```python
import functools
import jax
import jax.numpy as jnp
import numpy as np
from jax import lax
from jax.experimental import pallas as pl
from jax.experimental.pallas import tpu as pltpu
from jax.sharding import PartitionSpec as P

time_step = 0.2
penalty = 0.5
stress_of = ((0, 5, 4), (5, 1, 3), (4, 3, 2))
voigt_pairs = ((0, 0), (1, 1), (2, 2), (1, 2), (0, 2), (0, 1))
F32 = jnp.float32
BF16 = jnp.bfloat16
NODES, FACE, ROWS = 35, 15, 27 * 16
VROW = 40
KROW = 48


def tables():
    triangle = [(one, two) for one in range(5) for two in range(5 - one)]
    volume_nodes = [
        (one, two, three)
        for one in range(5)
        for two in range(5 - one)
        for three in range(5 - one - two)
    ]
    face_index = np.zeros((15, 4), np.int32)
    for entry, (a, b) in enumerate(triangle):
        for face, key in enumerate([(a, b, 0), (a, 0, b), (0, a, b), (a, b, 4 - a - b)]):
            face_index[entry, face] = volume_nodes.index(key)
    orders = [(0, 1, 2), (1, 2, 0), (2, 0, 1), (0, 2, 1), (2, 1, 0), (1, 0, 2)]
    turning = np.zeros((6, 15), np.int32)
    for orient_id, order in enumerate(orders):
        for entry, (a, b) in enumerate(triangle):
            coords = (a, b, 4 - a - b)
            turning[orient_id, entry] = triangle.index((coords[order[0]], coords[order[1]]))
    return face_index, turning


def split(x):
    high = x.astype(BF16)
    low = (x - high.astype(F32)).astype(BF16)
    return high, low


def dot(a, b):
    return jnp.dot(a, b, preferred_element_type=F32)


def dot_nt(a, b):
    return lax.dot_general(a, b, (((1,), (1,)), ((), ())), preferred_element_type=F32)


def pad_rows(x, rows):
    return jnp.concatenate([x, jnp.zeros((rows - x.shape[0],) + x.shape[1:], x.dtype)], axis=0)


def one_hot(ids, count, start=0):
    rows = lax.broadcasted_iota(jnp.int32, (count, ids.shape[1]), 0) + start
    return jnp.where(rows == ids, 1.0, 0.0).astype(BF16)


def turn_rows(turning, orient_row):
    lanes = orient_row.shape[1]
    rows = lax.broadcasted_iota(jnp.int32, (16, lanes), 0)
    result = rows
    for orient_id in range(1, 6):
        table = jnp.zeros((16, lanes), jnp.int32)
        for m in range(15):
            table = jnp.where(rows == m, int(turning[orient_id, m]), table)
        result = jnp.where(orient_row == orient_id, table, result)
    return result


def rotate(x, index):
    first, second = x[0:8], x[8:16]
    halves = []
    for h in range(2):
        part = index[8 * h : 8 * h + 8]
        inside = part & 7
        a = jnp.take_along_axis(first, inside, axis=0)
        b = jnp.take_along_axis(second, inside, axis=0)
        halves.append(jnp.where(part < 8, a, b))
    return jnp.concatenate(halves, axis=0)


def send_kernel(q0_ref, q1_ref, q2_ref, select_ref, send_ref, high_ref, low_ref, sent_ref):
    elements = q0_ref.shape[2]
    select = select_ref[...]
    for s, ref in enumerate((q0_ref, q1_ref, q2_ref)):
        for c in range(9):
            high, low = split(pad_rows(ref[c], KROW))
            trace = dot(select, jnp.concatenate([high, low], axis=0))
            t_high, t_low = split(trace)
            row = (s * 9 + c) * 16
            for f in range(4):
                high_ref[row : row + 16, f * elements : (f + 1) * elements] = t_high[
                    16 * f : 16 * f + 16
                ]
                low_ref[row : row + 16, f * elements : (f + 1) * elements] = t_low[
                    16 * f : 16 * f + 16
                ]
    picked = one_hot(send_ref[...], 4 * elements)
    sent = dot(high_ref[...], picked) + dot(low_ref[...], picked)
    sent_ref[...] = sent.T


def spread_kernel(coarse_ref, out_ref):
    width = coarse_ref.shape[1]
    rows = out_ref.shape[1]
    padded = pad_rows(coarse_ref[...], 4 * rows)
    for s in range(rows):
        for j in range(4):
            row = padded[4 * s + j : 4 * s + j + 1]
            out_ref[:, s, j * width : (j + 1) * width] = jnp.broadcast_to(
                row, (out_ref.shape[0], width)
            )


def own_kernel(
    turning,
    q0_ref,
    q1_ref,
    q2_ref,
    model_ref,
    geometry_ref,
    neighbor_ref,
    orient_ref,
    derivative_ref,
    lift_ref,
    prolong_ref,
    high_ref,
    low_ref,
    own_ref,
    vol0_ref,
    vol1_ref,
    vol2_ref,
    lift_out,
    prolong_out,
    restrict_out,
    left_ref,
    rows_ref,
):
    elements = q0_ref.shape[2]
    left_ref[...] = jnp.zeros_like(left_ref)
    for k in range(3):
        high, low = split(derivative_ref[k])
        r = k * VROW
        left_ref[r : r + NODES, 0:NODES] = high.astype(F32)
        left_ref[r : r + NODES, KROW : KROW + NODES] = high.astype(F32)
        left_ref[r : r + NODES, 2 * KROW : 2 * KROW + NODES] = low.astype(F32)
    left = left_ref[...].astype(BF16)
    rows_ref[...] = jnp.zeros_like(rows_ref)
    for f in range(4):
        rows_ref[16 * f : 16 * f + FACE, 0:NODES] = lift_ref[:, f, :]
    turned = rows_ref[...].T
    high, low = split(turned[0:VROW, 0:64])
    lift_out[...] = jnp.concatenate([high, high, low], axis=1)
    rows_ref[...] = jnp.zeros_like(rows_ref)
    rows_ref[0:80, 0:NODES] = prolong_ref[...].reshape(80, NODES)
    plain = rows_ref[...]
    high, low = split(plain[0:80, 0:KROW])
    restrict_out[...] = jnp.concatenate([high, high, low], axis=1)
    turned = plain.T
    high, low = split(turned[0:VROW, 0:80])
    prolong_out[...] = jnp.concatenate([high, high, low], axis=1)

    geometry = geometry_ref[...]
    for s, (ref, out) in enumerate(
        ((q0_ref, vol0_ref), (q1_ref, vol1_ref), (q2_ref, vol2_ref))
    ):
        local = []
        for c in range(9):
            high, low = split(pad_rows(ref[c], KROW))
            local.append(dot(left, jnp.concatenate([high, low, high], axis=0)))

        def grad(c, i):
            total = None
            for k in range(3):
                term = geometry[3 * i + k : 3 * i + k + 1] * local[c][k * VROW : k * VROW + VROW]
                total = term if total is None else total + term
            return total[0:NODES]

        terms = []
        for i in range(3):
            terms.append(sum(grad(3 + stress_of[i][j], j) for j in range(3)))
        for i, j in voigt_pairs:
            terms.append(2.0 * grad(i, i) if i == j else grad(j, i) + grad(i, j))
        if s == 0:
            for c in range(9):
                out[c] = terms[c]
        else:
            trace = (0.5 * model_ref[1]) * (terms[3] + terms[4] + terms[5])
            for c in range(9):
                value = (model_ref[0] if c < 3 else model_ref[2]) * terms[c]
                if 3 <= c < 6:
                    value = value + trace
                out[c] = ref[c] + time_step * value

    for f in range(4):
        lanes = slice(f * elements, (f + 1) * elements)
        picked = one_hot(neighbor_ref[f : f + 1], 4 * elements)
        outer = dot(high_ref[...], picked) + dot(low_ref[...], picked)
        index = turn_rows(turning, orient_ref[f : f + 1])
        for cs in range(27):
            r = slice(16 * cs, 16 * cs + 16)
            inner = high_ref[r, lanes].astype(F32) + low_ref[r, lanes].astype(F32)
            own_ref[r, lanes] = rotate(outer[r], index) - inner


def join_kernel(
    turning,
    recv_ref,
    coarse_ref,
    neighbor_ref,
    orient_ref,
    own_ref,
    vol0_ref,
    vol1_ref,
    vol2_ref,
    lift_ref,
    prolong_ref,
    restrict_ref,
    model_ref,
    normals_ref,
    scale_ref,
    observe_ref,
    owner_ref,
    local_ref,
    child_ref,
    delta_ref,
    adjoint_ref,
    message_ref,
    jump_ref,
    spread_ref,
):
    elements = model_ref.shape[2]
    devices = coarse_ref.shape[0]
    width = coarse_ref.shape[2] // 4
    slots = recv_ref.shape[0]
    received = recv_ref[...].T
    high, low = split(received)
    received = jnp.concatenate([high, low], axis=1)
    for f in range(4):
        lanes = slice(f * elements, (f + 1) * elements)
        picked = one_hot(neighbor_ref[f : f + 1], slots, 4 * elements)
        outer = dot(received, jnp.concatenate([picked, picked], axis=0))
        index = turn_rows(turning, orient_ref[f : f + 1])
        for cs in range(27):
            r = slice(16 * cs, 16 * cs + 16)
            jump_ref[r, lanes] = own_ref[r, lanes] + rotate(outer[r], index)

    owner_hot = one_hot(owner_ref[...], devices)
    local_hot = jnp.where(
        lax.broadcasted_iota(jnp.int32, (width, elements), 0) == local_ref[...], 1.0, 0.0
    )
    child_hot = jnp.where(
        lax.broadcasted_iota(jnp.int32, (8, elements), 0) == child_ref[...], 1.0, 0.0
    )
    fetched = []
    for s in range(coarse_ref.shape[1]):
        high, low = split(coarse_ref[:, s, :].T)
        spread = dot(high, owner_hot) + dot(low, owner_hot)
        for j in range(4):
            block = spread[j * width : (j + 1) * width] * local_hot
            fetched.append(jnp.sum(block, axis=0, keepdims=True))
    prolong = prolong_ref[...]
    step_fine = []
    for p in range(3):
        masked = jnp.concatenate([fetched[10 * p + k] * child_hot for k in range(10)], axis=0)
        high, low = split(masked)
        step_fine.append(
            dot(prolong, jnp.concatenate([high, low, high], axis=0))[0:NODES]
        )

    lift = lift_ref[...]

    def lifted(pieces):
        high, low = split(jnp.concatenate(pieces, axis=0))
        return dot(lift, jnp.concatenate([high, low, high], axis=0))[0:NODES]

    def flux(s):
        scaled, normal = [], []
        for f in range(4):
            half = 0.5 * scale_ref[f : f + 1]
            scaled.append(half)
            normal.append([half * normals_ref[j, f : f + 1] for j in range(3)])

        def jump(c, f):
            r = (s * 9 + c) * 16
            return jump_ref[r : r + 16, f * elements : (f + 1) * elements]

        result = []
        for i in range(3):
            result.append(
                lifted(
                    [
                        sum(normal[f][j] * jump(3 + stress_of[i][j], f) for j in range(3))
                        for f in range(4)
                    ]
                )
            )
        for i, j in voigt_pairs:
            if i == j:
                result.append(lifted([(2.0 * normal[f][i]) * jump(i, f) for f in range(4)]))
            else:
                result.append(
                    lifted(
                        [
                            normal[f][i] * jump(j, f) + normal[f][j] * jump(i, f)
                            for f in range(4)
                        ]
                    )
                )
        if s == 0:
            return result, None
        return result, [lifted([scaled[f] * jump(c, f) for f in range(4)]) for c in range(9)]

    def apply(first, second, third, terms):
        trace = (0.5 * second) * (terms[3] + terms[4] + terms[5])
        values = []
        for c in range(9):
            value = (first if c < 3 else third) * terms[c]
            values.append(value + trace if 3 <= c < 6 else value)
        return values

    lift0, _ = flux(0)
    base = [vol0_ref[c] + lift0[c] for c in range(9)]
    terms, pen = flux(1)
    moved = apply(model_ref[0], model_ref[1], model_ref[2], terms)
    pushed = apply(step_fine[0], step_fine[1], step_fine[2], base)
    for c in range(9):
        delta_ref[c] = vol1_ref[c] + time_step * (moved[c] + pen[c] + pushed[c])
    terms, pen = flux(2)
    moved = apply(model_ref[0], model_ref[1], model_ref[2], terms)
    for c in range(9):
        adjoint_ref[c] = vol2_ref[c] + time_step * (
            moved[c] + pen[c] + observe_ref[...] * delta_ref[c]
        )
    grads = [
        time_step * sum(adjoint_ref[i] * base[i] for i in range(3)),
        (0.5 * time_step)
        * ((adjoint_ref[3] + adjoint_ref[4] + adjoint_ref[5]) * (base[3] + base[4] + base[5])),
        time_step * sum(adjoint_ref[c] * base[c] for c in range(3, 9)),
    ]
    owner_twice = jnp.concatenate([owner_hot, owner_hot], axis=1)
    spread_ref[...] = jnp.zeros_like(spread_ref)
    for p in range(3):
        high, low = split(pad_rows(grads[p], KROW))
        parts = dot(restrict_ref[...], jnp.concatenate([high, low, high], axis=0))
        for k in range(10):
            row = jnp.sum(parts[8 * k : 8 * k + 8] * child_hot, axis=0, keepdims=True)
            high, low = split(row * local_hot)
            at = (10 * p + k) * width
            spread_ref[at : at + width] = jnp.concatenate([high, low], axis=1)
    gathered = dot_nt(owner_twice, spread_ref[...])
    for s in range(message_ref.shape[1]):
        message_ref[:, s, :] = gathered[:, s * 4 * width : (s + 1) * 4 * width]


def sum_kernel(arrived_ref, reg_ref, coarse_ref, out_ref):
    width = coarse_ref.shape[1]
    total = jnp.sum(arrived_ref[...], axis=0)
    weighted = reg_ref[...] * coarse_ref[...]
    for row in range(coarse_ref.shape[0]):
        s, j = row // 4, row % 4
        out_ref[row : row + 1] = (
            total[s : s + 1, j * width : (j + 1) * width] + weighted[row : row + 1]
        )


def call(kernel, outs, scratch=(), name=None, flops=0, bytes_accessed=0):
    return pl.pallas_call(
        kernel,
        out_shape=outs,
        scratch_shapes=list(scratch),
        name=name,
        cost_estimate=pl.CostEstimate(
            flops=flops, bytes_accessed=bytes_accessed, transcendentals=0
        ),
    )


def body(
    state0,
    delta,
    adjoint,
    model,
    geometry,
    normals,
    face_scale,
    derivative,
    lift,
    prolong,
    coarse_step,
    reg_weight,
    observe,
    owner,
    coarse_local,
    child,
    neighbor,
    orient,
    send_face,
):
    face_index, turning = tables()
    elements = state0.shape[2]
    wave_size = lax.axis_size("wave")
    devices = lax.axis_size(("region", "wave"))
    sends = send_face.shape[0]
    block, width = coarse_step.shape
    packs = 8
    everyone = ("region", "wave")
    select = np.zeros((64, 2 * KROW), np.float32)
    for f in range(4):
        for m in range(FACE):
            select[16 * f + m, face_index[m, f]] = 1.0
            select[16 * f + m, KROW + face_index[m, f]] = 1.0
    shape = jax.ShapeDtypeStruct

    spread = call(spread_kernel, shape((devices, packs, 4 * width), F32), name="spread")(coarse_step)
    high, low, sent = call(
        send_kernel,
        (
            shape((ROWS, 4 * elements), BF16),
            shape((ROWS, 4 * elements), BF16),
            shape((sends, ROWS), F32),
        ),
        name="send",
        bytes_accessed=3 << 20,
        flops=1 << 28,
    )(state0, delta, adjoint, jnp.asarray(select, BF16), send_face.reshape(1, sends))
    coarse = lax.all_to_all(spread, everyone, split_axis=0, concat_axis=0, tiled=True)
    got = lax.all_to_all(
        sent.reshape(wave_size, sends // wave_size, ROWS),
        "wave",
        split_axis=0,
        concat_axis=0,
        tiled=True,
    ).reshape(sends, ROWS)
    state = shape((9, NODES, elements), F32)
    own, vol0, vol1, vol2, lift_left, prolong_left, restrict_left = call(
        functools.partial(own_kernel, turning),
        (
            shape((ROWS, 4 * elements), F32),
            state,
            state,
            state,
            shape((VROW, 192), BF16),
            shape((VROW, 240), BF16),
            shape((80, 3 * KROW), BF16),
        ),
        scratch=(pltpu.VMEM((3 * VROW, 3 * KROW), F32), pltpu.VMEM((128, 128), F32)),
        name="own",
        bytes_accessed=8 << 20,
        flops=1 << 32,
    )(
        state0,
        delta,
        adjoint,
        model,
        geometry,
        neighbor,
        orient,
        derivative,
        lift.transpose(2, 0, 1),
        prolong.transpose(2, 0, 1),
        high,
        low,
    )
    delta_next, adjoint_next, message = call(
        functools.partial(join_kernel, turning),
        (state, state, shape((devices, packs, 4 * width), F32)),
        scratch=(
            pltpu.VMEM((ROWS, 4 * elements), F32),
            pltpu.VMEM((packs * 4 * width, 2 * elements), BF16),
        ),
        name="join",
        bytes_accessed=8 << 20,
        flops=1 << 30,
    )(
        got,
        coarse,
        neighbor,
        orient,
        own,
        vol0,
        vol1,
        vol2,
        lift_left,
        prolong_left,
        restrict_left,
        model,
        normals,
        face_scale,
        observe,
        owner.reshape(1, elements),
        coarse_local.reshape(1, elements),
        child.reshape(1, elements),
    )
    arrived = lax.all_to_all(message, everyone, split_axis=0, concat_axis=0, tiled=True)
    hess_vec = call(sum_kernel, shape((block, width), F32), name="total")(
        arrived, reg_weight, coarse_step
    )
    return (delta_next, adjoint_next, hess_vec)


def solution(mesh):
    both = ("region", "wave")
    wide, flat = P(None, None, both), P(None, both)
    placed = (
        wide,
        wide,
        wide,
        wide,
        flat,
        wide,
        flat,
        P(),
        P(),
        P(),
        flat,
        flat,
        flat,
        P(both, None),
        P(both),
        P(both),
        flat,
        flat,
        P(both),
    )
    return jax.shard_map(
        body, mesh=mesh, in_specs=placed, out_specs=(wide, wide, flat), check_vma=False
    )
```

profile of v0, /device:TPU:0, one launch (start us, length us, event | category | flops | bytes accessed | tf_op | source)
XLA Modules:
  0.0 49.7 jit_solution(18164414962204086872)
XLA Ops:
  0.6 1.6 %spread.1 = f32[32,8,128]{2,1,0:T(8,128)} custom-call(f32[30,32]{1,0:T(8,128)} %coarse_ref.3), custom_call_target="tpu_custom_call" | custom-call | tf_op jit(solution)/shard_map/spread/pallas_call | solution.py:422
  2.3 7.3 %all-to-all-start.1 = ((f32[32,8,128]{2,1,0:T(8,128)}), f32[32,8,128]{2,1,0:T(8,128)S(1)}, u32[]{:S(2)}, u32[]{:S(2)}) async-start(f32[32,8,128]{2,1,0:T(8,128)} %spread.1), calls=%async_computation.1 | async-start | bytes 262144 | tf_op jit(solution)/shard_map/all_to_all | solution.py:434
  9.6 3.0 %send.1 = (bf16[432,1024]{1,0:T(8,128)(2,1)}, bf16[432,1024]{1,0:T(8,128)(2,1)}, f32[128,432]{1,0:T(8,128)}) custom-call(f32[9,35,256]{2,1,0:T(8,128)} %q0_ref.3, f32[9,35,256]{2,1,0:T(8,128)} %q1_ref.3, f32[9,35,256]{2,1,0:T(8,128)} %q2_ref.3, bf16[64,96]{1,0:T(8,128)(2,1)} %constant.2.clone.select_ref, s32[1,128]{1,0:T(1,128)} %bitcast.10), custom_call_target="tpu_custom_call" | custom-call | flops 268435456 | bytes 3145728 | tf_op jit(solution)/shard_map/send/pallas_call | solution.py:423
  12.6 5.2 %all-to-all-done.1.coarse_ref = f32[32,8,128]{2,1,0:T(8,128)S(1)} async-done(((f32[32,8,128]{2,1,0:T(8,128)}), f32[32,8,128]{2,1,0:T(8,128)S(1)}, u32[]{:S(2)}, u32[]{:S(2)}) %all-to-all-start.1) | async-done | bytes 131104 | tf_op jit(solution)/shard_map/all_to_all | solution.py:434
  17.8 0.0 copy-start.1
  17.8 3.4 %all-to-all-start = ((f32[8,16,432]{2,1,0:T(8,128)}), f32[8,16,432]{2,1,0:T(8,128)S(1)}, u32[]{:S(2)}, u32[]{:S(2)}) async-start(f32[8,16,432]{2,1,0:T(8,128)} %bitcast.9), calls=%async_computation | async-start | bytes 524288 | tf_op jit(solution)/shard_map/all_to_all | solution.py:435
  21.2 6.4 %own.1 = (f32[432,1024]{1,0:T(8,128)}, f32[9,35,256]{2,1,0:T(8,128)}, f32[9,35,256]{2,1,0:T(8,128)}, f32[9,35,256]{2,1,0:T(8,128)}, bf16[40,192]{1,0:T(8,128)(2,...) custom-call(f32[9,35,256]{2,1,0:T(8,128)} %q0_ref.3, f32[9,35,256]{2,1,0:T(8,128)} %q1_ref.3, f32[9,35,256]{2,1,0:T(8,128)} %q2_ref.3, ...), custom_call_target="tpu_custom_call" | custom-call | flops 4294967296 | bytes 8388608 | tf_op jit(solution)/shard_map/own/pallas_call | solution.py:443
  27.6 0.0 copy-done.1
  27.6 3.2 %all-to-all-done = f32[8,16,432]{2,1,0:T(8,128)S(1)} async-done(((f32[8,16,432]{2,1,0:T(8,128)}), f32[8,16,432]{2,1,0:T(8,128)S(1)}, u32[]{:S(2)}, u32[]{:S(2)}) %all-to-all-start) | async-done | bytes 221216 | tf_op jit(solution)/shard_map/all_to_all | solution.py:435
  30.8 0.0 copy-start
  30.8 0.7 %copy-done = f32[8,16,432]{2,1,0:T(8,128)} copy-done((f32[8,16,432]{2,1,0:T(8,128)}, f32[8,16,432]{2,1,0:T(8,128)S(1)}, u32[]{:S(2)}) %copy-start) | copy-done | bytes 221208
  31.5 5.1 %join.1 = (f32[9,35,256]{2,1,0:T(8,128)}, f32[9,35,256]{2,1,0:T(8,128)}, f32[32,8,128]{2,1,0:T(8,128)}) custom-call(f32[128,432]{1,0:T(8,128)} %bitcast.8, f32[32,8,128]{2,1,0:T(8,128)} %copy-done.1, s32[4,256]{1,0:T(4,128)} %neighbor_ref.3, s32[4,256]{1,0:T(4,128)} %orient_ref.3, f32[432,1024]{1,0:T(8,128)} %get-tuple-element.19.own_ref, ...), custom_call_target="tpu_custom_call" | custom-call | flops 1073741824 | bytes 8388608 | tf_op jit(solution)/shard_map/join/pallas_call | solution.py:472
  36.6 11.4 %all_to_all.15.arrived_ref = f32[32,8,128]{2,1,0:T(8,128)} all-to-all(f32[32,8,128]{2,1,0:T(8,128)} %get-tuple-element.28), channel_id=1, replica_groups=mesh['region'=4,'wave'=8] {'region','wave'}, dimensions={0} | all-to-all | bytes 262144 | tf_op jit(solution)/shard_map/all_to_all | solution.py:502
  48.0 1.7 %total.1 = f32[30,32]{1,0:T(8,128)} custom-call(f32[32,8,128]{2,1,0:T(8,128)} %all_to_all.15.arrived_ref, f32[30,32]{1,0:T(8,128)} %reg_ref.1, f32[30,32]{1,0:T(8,128)} %coarse_ref.3), custom_call_target="tpu_custom_call" | custom-call | tf_op jit(solution)/shard_map/total/pallas_call | solution.py:503
Async XLA Ops:
  2.3 15.5 %all-to-all-start.1 = ((f32[32,8,128]{2,1,0:T(8,128)}), f32[32,8,128]{2,1,0:T(8,128)S(1)}, u32[]{:S(2)}, u32[]{:S(2)}) async-start(f32[32,8,128]{2,1,0:T(8,128)} %spread.1), calls=%async_computation.1 | async-start | bytes 262144 | tf_op jit(solution)/shard_map/all_to_all | solution.py:434
  17.8 9.8 %copy-start.1 = (f32[32,8,128]{2,1,0:T(8,128)}, f32[32,8,128]{2,1,0:T(8,128)S(1)}, u32[]{:S(2)}) copy-start(f32[32,8,128]{2,1,0:T(8,128)S(1)} %all-to-all-done.1.coarse_ref) | copy-start | bytes 393220
  17.8 13.1 %all-to-all-start = ((f32[8,16,432]{2,1,0:T(8,128)}), f32[8,16,432]{2,1,0:T(8,128)S(1)}, u32[]{:S(2)}, u32[]{:S(2)}) async-start(f32[8,16,432]{2,1,0:T(8,128)} %bitcast.9), calls=%async_computation | async-start | bytes 524288 | tf_op jit(solution)/shard_map/all_to_all | solution.py:435
  30.8 0.7 %copy-start = (f32[8,16,432]{2,1,0:T(8,128)}, f32[8,16,432]{2,1,0:T(8,128)S(1)}, u32[]{:S(2)}) copy-start(f32[8,16,432]{2,1,0:T(8,128)S(1)} %all-to-all-done) | copy-start | bytes 663556
where the time goes:
time: 50.2 us; the launch traced here: 49.7 us
  Pallas kernels  17.8 us (35%)
  blocking collectives  11.4 us (23%)
  starting transfers between devices  10.7 us (21%)
  waiting for transfers between devices  8.43 us (17%)
  local copies, waits for them, and re-layouts  0.71 us (1%)
  between operations  0.66 us (1%)
    all_to_all x1, blocking collectives, body(): lax.all_to_all(message, everyone, split_axis=0, concat_axis=0, tiled=True)  11.4 us
    all_to_all x1, starting transfers between devices, body(): lax.all_to_all(spread, everyone, split_axis=0, concat_axis=0, tiled=True)  7.33 us
    pallas_call x1, Pallas kernels, body(): call(functools.partial(own_kernel, turning), (shape((ROWS, 4 * elements),...  6.38 us
    all_to_all x1, waiting for transfers between devices, body(): lax.all_to_all(spread, everyone, split_axis=0, concat_axis=0, tiled=True)  5.2 us
    pallas_call x1, Pallas kernels, body(): call(functools.partial(join_kernel, turning), (state, state, shape((devic...  5.09 us
    all_to_all x1, starting transfers between devices, body(): lax.all_to_all(sent.reshape(wave_size, sends // wave_size, ROWS), 'wave',...  3.41 us
    all_to_all x1, waiting for transfers between devices, body(): lax.all_to_all(sent.reshape(wave_size, sends // wave_size, ROWS), 'wave',...  3.24 us
    pallas_call x1, Pallas kernels, body(): call(send_kernel, (shape((ROWS, 4 * elements), BF16), shape((ROWS, 4 * el...  2.96 us
  transfers between devices with their start and end apart: 2, of which 2 were waited for; matrix products, arithmetic and copies ran while one was open for 0% of the time, Pallas kernels for 13%

commit v1 on v0

--- a/solution.py
+++ b/solution.py
@@ -86,37 +86,91 @@
     return jnp.concatenate(halves, axis=0)
 
 
-def send_kernel(q0_ref, q1_ref, q2_ref, select_ref, send_ref, high_ref, low_ref, sent_ref):
-    elements = q0_ref.shape[2]
+def fetch(pairs, sems):
+    copies = []
+    for index, (source, target) in enumerate(pairs):
+        copy = pltpu.make_async_copy(source, target, sems.at[index])
+        copy.start()
+        copies.append(copy)
+    return copies
+
+
+def send_kernel(
+    q0_hbm,
+    q1_hbm,
+    q2_hbm,
+    select_hbm,
+    send_hbm,
+    coarse_hbm,
+    high_out,
+    low_out,
+    sent_ref,
+    q_ref,
+    select_ref,
+    send_ref,
+    coarse_ref,
+    high_ref,
+    low_ref,
+    in_sems,
+    out_sems,
+):
+    elements = q_ref.shape[3]
+    slots = sent_ref.shape[1]
+    block, width = coarse_ref.shape
+    sources = (q0_hbm, q1_hbm, q2_hbm)
+    copies = fetch(
+        [(select_hbm, select_ref)]
+        + [(sources[s], q_ref.at[s]) for s in range(3)]
+        + [(send_hbm, send_ref), (coarse_hbm, coarse_ref)],
+        in_sems,
+    )
+    copies[0].wait()
     select = select_ref[...]
-    for s, ref in enumerate((q0_ref, q1_ref, q2_ref)):
+    written = []
+    for s in range(3):
+        copies[1 + s].wait()
         for c in range(9):
-            high, low = split(pad_rows(ref[c], KROW))
+            high, low = split(pad_rows(q_ref[s, c], KROW))
             trace = dot(select, jnp.concatenate([high, low], axis=0))
             t_high, t_low = split(trace)
             row = (s * 9 + c) * 16
             for f in range(4):
-                high_ref[row : row + 16, f * elements : (f + 1) * elements] = t_high[
-                    16 * f : 16 * f + 16
-                ]
-                low_ref[row : row + 16, f * elements : (f + 1) * elements] = t_low[
-                    16 * f : 16 * f + 16
-                ]
+                lanes = slice(f * elements, (f + 1) * elements)
+                high_ref[row : row + 16, lanes] = t_high[16 * f : 16 * f + 16]
+                low_ref[row : row + 16, lanes] = t_low[16 * f : 16 * f + 16]
+        rows = pl.ds(s * 144, 144)
+        written += fetch(
+            [(high_ref.at[rows], high_out.at[rows]), (low_ref.at[rows], low_out.at[rows])],
+            out_sems.at[s],
+        )
+    copies[4].wait()
     picked = one_hot(send_ref[...], 4 * elements)
     sent = dot(high_ref[...], picked) + dot(low_ref[...], picked)
-    sent_ref[...] = sent.T
-
-
-def spread_kernel(coarse_ref, out_ref):
-    width = coarse_ref.shape[1]
-    rows = out_ref.shape[1]
-    padded = pad_rows(coarse_ref[...], 4 * rows)
-    for s in range(rows):
-        for j in range(4):
-            row = padded[4 * s + j : 4 * s + j + 1]
-            out_ref[:, s, j * width : (j + 1) * width] = jnp.broadcast_to(
-                row, (out_ref.shape[0], width)
-            )
+    sent_ref[:, :, 0:ROWS] = sent.T.reshape(sent_ref.shape[0], slots, ROWS)
+    copies[5].wait()
+    pieces = spare(block, slots)
+    padded = pad_rows(coarse_ref[...], pieces * slots)
+    for h in range(pieces):
+        part = padded[h * slots : (h + 1) * slots]
+        for w in range(sent_ref.shape[0]):
+            sent_ref[w, :, ROWS + h * width : ROWS + (h + 1) * width] = part
+    for copy in written:
+        copy.wait()
+
+
+def spare(block, slots):
+    return -(-block // slots)
+
+
+def pick_kernel(got_ref, out_ref):
+    waves, slots, _ = got_ref.shape
+    rows = out_ref.shape[0]
+    width = out_ref.shape[1] // waves
+    for w in range(waves):
+        for h in range(rows // slots):
+            out_ref[h * slots : (h + 1) * slots, w * width : (w + 1) * width] = got_ref[
+                w, :, ROWS + h * width : ROWS + (h + 1) * width
+            ]
 
 
 def own_kernel(
@@ -210,39 +264,56 @@
             own_ref[r, lanes] = rotate(outer[r], index) - inner
 
 
-def join_kernel(
+def model_terms(first, second, third, terms):
+    trace = (0.5 * second) * (terms[3] + terms[4] + terms[5])
+    values = []
+    for c in range(9):
+        value = (first if c < 3 else third) * terms[c]
+        values.append(value + trace if 3 <= c < 6 else value)
+    return values
+
+
+def jump_kernel(
     turning,
-    recv_ref,
-    coarse_ref,
-    neighbor_ref,
-    orient_ref,
+    got_ref,
+    neighbor_hbm,
+    orient_hbm,
     own_ref,
+    lift_ref,
+    normals_hbm,
+    scale_hbm,
     vol0_ref,
     vol1_ref,
     vol2_ref,
-    lift_ref,
-    prolong_ref,
-    restrict_ref,
-    model_ref,
+    model_hbm,
+    base_ref,
+    moved_ref,
+    backed_ref,
+    neighbor_ref,
+    orient_ref,
     normals_ref,
     scale_ref,
-    observe_ref,
-    owner_ref,
-    local_ref,
-    child_ref,
-    delta_ref,
-    adjoint_ref,
-    message_ref,
+    model_ref,
     jump_ref,
-    spread_ref,
+    sems,
 ):
     elements = model_ref.shape[2]
-    devices = coarse_ref.shape[0]
-    width = coarse_ref.shape[2] // 4
-    slots = recv_ref.shape[0]
-    received = recv_ref[...].T
+    slots = got_ref.shape[0] * got_ref.shape[1]
+    copies = fetch(
+        [
+            (neighbor_hbm, neighbor_ref),
+            (orient_hbm, orient_ref),
+            (normals_hbm, normals_ref),
+            (scale_hbm, scale_ref),
+            (model_hbm, model_ref),
+        ],
+        sems,
+    )
+    received = got_ref[...].reshape(slots, got_ref.shape[2])[:, 0:ROWS].T
     high, low = split(received)
     received = jnp.concatenate([high, low], axis=1)
+    for copy in copies[0:2]:
+        copy.wait()
     for f in range(4):
         lanes = slice(f * elements, (f + 1) * elements)
         picked = one_hot(neighbor_ref[f : f + 1], slots, 4 * elements)
@@ -251,43 +322,21 @@
         for cs in range(27):
             r = slice(16 * cs, 16 * cs + 16)
             jump_ref[r, lanes] = own_ref[r, lanes] + rotate(outer[r], index)
-
-    owner_hot = one_hot(owner_ref[...], devices)
-    local_hot = jnp.where(
-        lax.broadcasted_iota(jnp.int32, (width, elements), 0) == local_ref[...], 1.0, 0.0
-    )
-    child_hot = jnp.where(
-        lax.broadcasted_iota(jnp.int32, (8, elements), 0) == child_ref[...], 1.0, 0.0
-    )
-    fetched = []
-    for s in range(coarse_ref.shape[1]):
-        high, low = split(coarse_ref[:, s, :].T)
-        spread = dot(high, owner_hot) + dot(low, owner_hot)
-        for j in range(4):
-            block = spread[j * width : (j + 1) * width] * local_hot
-            fetched.append(jnp.sum(block, axis=0, keepdims=True))
-    prolong = prolong_ref[...]
-    step_fine = []
-    for p in range(3):
-        masked = jnp.concatenate([fetched[10 * p + k] * child_hot for k in range(10)], axis=0)
-        high, low = split(masked)
-        step_fine.append(
-            dot(prolong, jnp.concatenate([high, low, high], axis=0))[0:NODES]
-        )
-
+    for copy in copies[2:]:
+        copy.wait()
     lift = lift_ref[...]
 
     def lifted(pieces):
         high, low = split(jnp.concatenate(pieces, axis=0))
         return dot(lift, jnp.concatenate([high, low, high], axis=0))[0:NODES]
 
+    scaled, normal = [], []
+    for f in range(4):
+        half = 0.5 * scale_ref[f : f + 1]
+        scaled.append(half)
+        normal.append([half * normals_ref[j, f : f + 1] for j in range(3)])
+
     def flux(s):
-        scaled, normal = [], []
-        for f in range(4):
-            half = 0.5 * scale_ref[f : f + 1]
-            scaled.append(half)
-            normal.append([half * normals_ref[j, f : f + 1] for j in range(3)])
-
         def jump(c, f):
             r = (s * 9 + c) * 16
             return jump_ref[r : r + 16, f * elements : (f + 1) * elements]
@@ -318,35 +367,101 @@
             return result, None
         return result, [lifted([scaled[f] * jump(c, f) for f in range(4)]) for c in range(9)]
 
-    def apply(first, second, third, terms):
-        trace = (0.5 * second) * (terms[3] + terms[4] + terms[5])
-        values = []
+    terms, _ = flux(0)
+    for c in range(9):
+        base_ref[c] = vol0_ref[c] + terms[c]
+    for s, vol_ref, out in ((1, vol1_ref, moved_ref), (2, vol2_ref, backed_ref)):
+        terms, pen = flux(s)
+        values = model_terms(model_ref[0], model_ref[1], model_ref[2], terms)
         for c in range(9):
-            value = (first if c < 3 else third) * terms[c]
-            values.append(value + trace if 3 <= c < 6 else value)
-        return values
-
-    lift0, _ = flux(0)
-    base = [vol0_ref[c] + lift0[c] for c in range(9)]
-    terms, pen = flux(1)
-    moved = apply(model_ref[0], model_ref[1], model_ref[2], terms)
-    pushed = apply(step_fine[0], step_fine[1], step_fine[2], base)
+            out[c] = vol_ref[c] + time_step * (values[c] + pen[c])
+
+
+def step_kernel(
+    regions,
+    *refs,
+):
+    blocks, refs = refs[:regions], refs[regions:]
+    (
+        base_ref,
+        moved_ref,
+        backed_ref,
+        prolong_ref,
+        restrict_ref,
+        observe_hbm,
+        owner_hbm,
+        local_hbm,
+        child_hbm,
+        delta_ref,
+        adjoint_ref,
+        message_ref,
+        observe_ref,
+        owner_ref,
+        local_ref,
+        child_ref,
+        spread_ref,
+        sems,
+    ) = refs
+    elements = observe_ref.shape[1]
+    devices = message_ref.shape[0]
+    width = message_ref.shape[2] // 4
+    share = blocks[0].shape[1]
+    waves = share // width
+    copies = fetch(
+        [
+            (owner_hbm, owner_ref),
+            (local_hbm, local_ref),
+            (child_hbm, child_ref),
+            (observe_hbm, observe_ref),
+        ],
+        sems,
+    )
+    for copy in copies:
+        copy.wait()
+    owner, local = owner_ref[...], local_ref[...]
+    away = owner // waves - lax.axis_index("region")
+    away = jnp.where(away < 0, away + regions, away)
+    place = away * share + lax.rem(owner, waves) * width + local
+    total = None
+    for s in range(regions):
+        high, low = split(blocks[s][...])
+        hot = one_hot(place, share, s * share)
+        part = dot(jnp.concatenate([high, low], axis=0), hot)
+        total = part if total is None else total + part
+    fetched = total[0:32] + total[32:64]
+    owner_hot = one_hot(owner, devices)
+    local_hot = jnp.where(
+        lax.broadcasted_iota(jnp.int32, (width, elements), 0) == local, 1.0, 0.0
+    )
+    child_hot = jnp.where(
+        lax.broadcasted_iota(jnp.int32, (8, elements), 0) == child_ref[...], 1.0, 0.0
+    )
+    prolong = prolong_ref[...]
+    step_fine = []
+    for p in range(3):
+        masked = jnp.concatenate(
+            [fetched[10 * p + k : 10 * p + k + 1] * child_hot for k in range(10)], axis=0
+        )
+        high, low = split(masked)
+        step_fine.append(dot(prolong, jnp.concatenate([high, low, high], axis=0))[0:NODES])
+    base = [base_ref[c] for c in range(9)]
+    pushed = model_terms(step_fine[0], step_fine[1], step_fine[2], base)
+    observe = time_step * observe_ref[...]
+    ahead = []
     for c in range(9):
-        delta_ref[c] = vol1_ref[c] + time_step * (moved[c] + pen[c] + pushed[c])
-    terms, pen = flux(2)
-    moved = apply(model_ref[0], model_ref[1], model_ref[2], terms)
-    for c in range(9):
-        adjoint_ref[c] = vol2_ref[c] + time_step * (
-            moved[c] + pen[c] + observe_ref[...] * delta_ref[c]
-        )
+        value = moved_ref[c] + time_step * pushed[c]
+        delta_ref[c] = value
+        value = backed_ref[c] + observe * value
+        adjoint_ref[c] = value
+        ahead.append(value)
     grads = [
-        time_step * sum(adjoint_ref[i] * base[i] for i in range(3)),
-        (0.5 * time_step)
-        * ((adjoint_ref[3] + adjoint_ref[4] + adjoint_ref[5]) * (base[3] + base[4] + base[5])),
-        time_step * sum(adjoint_ref[c] * base[c] for c in range(3, 9)),
+        time_step * sum(ahead[i] * base[i] for i in range(3)),
+        (0.5 * time_step) * ((ahead[3] + ahead[4] + ahead[5]) * (base[3] + base[4] + base[5])),
+        time_step * sum(ahead[c] * base[c] for c in range(3, 9)),
     ]
     owner_twice = jnp.concatenate([owner_hot, owner_hot], axis=1)
-    spread_ref[...] = jnp.zeros_like(spread_ref)
+    used = 30 * width
+    spread_ref[used:] = jnp.zeros((spread_ref.shape[0] - used, 2 * elements), BF16)
     for p in range(3):
         high, low = split(pad_rows(grads[p], KROW))
         parts = dot(restrict_ref[...], jnp.concatenate([high, low, high], axis=0))
@@ -371,16 +486,44 @@
         )
 
 
-def call(kernel, outs, scratch=(), name=None, flops=0, bytes_accessed=0):
-    return pl.pallas_call(
+HBM, VMEM = pltpu.MemorySpace.HBM, pltpu.MemorySpace.VMEM
+
+
+def call(kernel, name, ins, outs, scratch=(), limit=16 << 20, flops=0, bytes_accessed=0):
+    specs = {
+        "h": pl.BlockSpec(memory_space=HBM),
+        "v": pl.BlockSpec(memory_space=VMEM),
+        "w": pl.BlockSpec(),
+    }
+    shapes = []
+    for how, shape, dtype in outs:
+        if how == "h":
+            shapes.append(HBM(shape, dtype))
+        elif how == "v":
+            shapes.append(VMEM(shape, dtype))
+        else:
+            shapes.append(jax.ShapeDtypeStruct(shape, dtype))
+    run = pl.pallas_call(
         kernel,
-        out_shape=outs,
+        out_shape=tuple(shapes),
+        in_specs=[specs[how] for how in ins],
+        out_specs=tuple(specs[how] for how, _, _ in outs),
         scratch_shapes=list(scratch),
         name=name,
         cost_estimate=pl.CostEstimate(
             flops=flops, bytes_accessed=bytes_accessed, transcendentals=0
         ),
-    )
+        compiler_params=pltpu.CompilerParams(vmem_limit_bytes=limit),
+    )
+
+    def placed(*operands):
+        fixed = [
+            pltpu.with_memory_space_constraint(x, VMEM if how == "v" else HBM)
+            for how, x in zip(ins, operands, strict=True)
+        ]
+        return run(*fixed)
+
+    return placed
 
 
 def body(
@@ -417,42 +560,51 @@
         for m in range(FACE):
             select[16 * f + m, face_index[m, f]] = 1.0
             select[16 * f + m, KROW + face_index[m, f]] = 1.0
-    shape = jax.ShapeDtypeStruct
-
-    spread = call(spread_kernel, shape((devices, packs, 4 * width), F32), name="spread")(coarse_step)
+    slots = sends // wave_size
+    regions = devices // wave_size
+    lanes = ROWS + spare(block, slots) * width
+    lanes = -(-lanes // 128) * 128
+    faces = 4 * elements
+    state = (9, NODES, elements)
+
     high, low, sent = call(
         send_kernel,
+        "send",
+        "hhhhhh",
         (
-            shape((ROWS, 4 * elements), BF16),
-            shape((ROWS, 4 * elements), BF16),
-            shape((sends, ROWS), F32),
+            ("h", (ROWS, faces), BF16),
+            ("h", (ROWS, faces), BF16),
+            ("w", (wave_size, slots, lanes), F32),
         ),
-        name="send",
+        scratch=(
+            pltpu.VMEM((3, 9, NODES, elements), F32),
+            pltpu.VMEM(select.shape, BF16),
+            pltpu.VMEM((1, sends), jnp.int32),
+            pltpu.VMEM((block, width), F32),
+            pltpu.VMEM((ROWS, faces), BF16),
+            pltpu.VMEM((ROWS, faces), BF16),
+            pltpu.SemaphoreType.DMA((6,)),
+            pltpu.SemaphoreType.DMA((3, 2)),
+        ),
         bytes_accessed=3 << 20,
         flops=1 << 28,
-    )(state0, delta, adjoint, jnp.asarray(select, BF16), send_face.reshape(1, sends))
-    coarse = lax.all_to_all(spread, everyone, split_axis=0, concat_axis=0, tiled=True)
-    got = lax.all_to_all(
-        sent.reshape(wave_size, sends // wave_size, ROWS),
-        "wave",
-        split_axis=0,
-        concat_axis=0,
-        tiled=True,
-    ).reshape(sends, ROWS)
-    state = shape((9, NODES, elements), F32)
+    )(state0, delta, adjoint, jnp.asarray(select, BF16), send_face.reshape(1, sends), coarse_step)
+    got = lax.all_to_all(sent, "wave", split_axis=0, concat_axis=0, tiled=True)
     own, vol0, vol1, vol2, lift_left, prolong_left, restrict_left = call(
         functools.partial(own_kernel, turning),
+        "own",
+        "w" * 12,
         (
-            shape((ROWS, 4 * elements), F32),
-            state,
-            state,
-            state,
-            shape((VROW, 192), BF16),
-            shape((VROW, 240), BF16),
-            shape((80, 3 * KROW), BF16),
+            ("v", (ROWS, faces), F32),
+            ("v", state, F32),
+            ("v", state, F32),
+            ("v", state, F32),
+            ("v", (VROW, 192), BF16),
+            ("v", (VROW, 240), BF16),
+            ("v", (80, 3 * KROW), BF16),
         ),
         scratch=(pltpu.VMEM((3 * VROW, 3 * KROW), F32), pltpu.VMEM((128, 128), F32)),
-        name="own",
+        limit=32 << 20,
         bytes_accessed=8 << 20,
         flops=1 << 32,
     )(
@@ -469,40 +621,61 @@
         high,
         low,
     )
+    rows = spare(block, slots) * slots
+    (near,) = call(pick_kernel, "pick", "v", (("v", (rows, wave_size * width), F32),), limit=4 << 20)(got)
+    blocks = [near]
+    for s in range(1, regions):
+        pairs = [(i, (i - s) % regions) for i in range(regions)]
+        blocks.append(lax.ppermute(near, "region", pairs))
+    base, moved, backed = call(
+        functools.partial(jump_kernel, turning),
+        "jump",
+        "vhh" + "v" + "v" + "hh" + "v" * 3 + "h",
+        (("v", state, F32),) * 3,
+        scratch=(
+            pltpu.VMEM((4, elements), jnp.int32),
+            pltpu.VMEM((4, elements), jnp.int32),
+            pltpu.VMEM((3, 4, elements), F32),
+            pltpu.VMEM((4, elements), F32),
+            pltpu.VMEM((3, NODES, elements), F32),
+            pltpu.VMEM((ROWS, faces), F32),
+            pltpu.SemaphoreType.DMA((5,)),
+        ),
+        bytes_accessed=8 << 20,
+        flops=1 << 31,
+    )(got, neighbor, orient, own, lift_left, normals, face_scale, vol0, vol1, vol2, model)
     delta_next, adjoint_next, message = call(
-        functools.partial(join_kernel, turning),
-        (state, state, shape((devices, packs, 4 * width), F32)),
+        functools.partial(step_kernel, regions),
+        "step",
+        "v" * (regions + 3) + "v" + "v" + "h" * 4,
+        (("w", state, F32), ("w", state, F32), ("v", (devices, packs, 4 * width), F32)),
         scratch=(
-            pltpu.VMEM((ROWS, 4 * elements), F32),
+            pltpu.VMEM((NODES, elements), F32),
+            pltpu.VMEM((1, elements), jnp.int32),
+            pltpu.VMEM((1, elements), jnp.int32),
+            pltpu.VMEM((1, elements), jnp.int32),
             pltpu.VMEM((packs * 4 * width, 2 * elements), BF16),
+            pltpu.SemaphoreType.DMA((4,)),
         ),
-        name="join",
-        bytes_accessed=8 << 20,
+        limit=12 << 20,
+        bytes_accessed=4 << 20,
         flops=1 << 30,
     )(
-        got,
-        coarse,
-        neighbor,
-        orient,
-        own,
-        vol0,
-        vol1,
-        vol2,
-        lift_left,
+        *blocks,
+        base,
+        moved,
+        backed,
         prolong_left,
         restrict_left,
-        model,
-        normals,
-        face_scale,
         observe,
         owner.reshape(1, elements),
         coarse_local.reshape(1, elements),
         child.reshape(1, elements),
     )
     arrived = lax.all_to_all(message, everyone, split_axis=0, concat_axis=0, tiled=True)
-    hess_vec = call(sum_kernel, shape((block, width), F32), name="total")(
-        arrived, reg_weight, coarse_step
-    )
+    (hess_vec,) = call(
+        sum_kernel, "total", "vvv", (("w", (block, width), F32),), limit=4 << 20
+    )(arrived, reg_weight, coarse_step)
     return (delta_next, adjoint_next, hess_vec)
 
 

time: 50.2 us -> 42 us (0.84)
  Pallas kernels: 17.8 us -> 14 us
  waiting for transfers between devices: 8.43 us -> 6.46 us
  blocking collectives: 11.4 us -> 10.6 us
  starting transfers between devices: 10.7 us -> 9.96 us
  local copies, waits for them, and re-layouts: 0.71 us -> 0.01 us
    all_to_all x2 -> x1, starting transfers between devices: 10.7 us -> 6.36 us  [body(): got = lax.all_to_all(sent, 'wave', split_axis=0, concat_axis=0, tiled=True)]
    all_to_all x2 -> x1, waiting for transfers between devices: 8.43 us -> 4.56 us  [body(): got = lax.all_to_all(sent, 'wave', split_axis=0, concat_axis=0, tiled=True)]
    pallas_call x5 -> x6, Pallas kernels: 17.8 us -> 14 us  [placed(): return run(*fixed)]
    ppermute x0 -> x3, starting transfers between devices: none -> 3.6 us  [body(): blocks.append(lax.ppermute(near, 'region', pairs))]
    ppermute x0 -> x3, waiting for transfers between devices: none -> 1.89 us  [body(): blocks.append(lax.ppermute(near, 'region', pairs))]
    all_to_all x1, blocking collectives: 11.4 us -> 10.6 us  [body(): lax.all_to_all(message, everyone, split_axis=0, concat_axis=0, tiled=True)]
    unnamed x4, local copies, waits for them, and re-layouts: 0.71 us -> 0.01 us
  transfers between devices with their start and end apart: 2 -> 4, of which waited for: 2 -> 3; matrix products, arithmetic and copies ran while one was open for 0% -> 0% of each run, Pallas kernels for 13% -> 18%
where the time goes in v1:
time: 42 us; the launch traced here: 41.7 us
  Pallas kernels  14 us (33%)
  blocking collectives  10.6 us (25%)
  starting transfers between devices  9.96 us (24%)
  waiting for transfers between devices  6.46 us (15%)
  between operations  0.68 us (2%)
    pallas_call x6, Pallas kernels, placed(): return run(*fixed)  14 us
    all_to_all x1, blocking collectives, body(): lax.all_to_all(message, everyone, split_axis=0, concat_axis=0, tiled=True)  10.6 us
    all_to_all x1, starting transfers between devices, body(): got = lax.all_to_all(sent, 'wave', split_axis=0, concat_axis=0, tiled=True)  6.36 us
    all_to_all x1, waiting for transfers between devices, body(): got = lax.all_to_all(sent, 'wave', split_axis=0, concat_axis=0, tiled=True)  4.56 us
    ppermute x3, starting transfers between devices, body(): blocks.append(lax.ppermute(near, 'region', pairs))  3.6 us
    ppermute x3, waiting for transfers between devices, body(): blocks.append(lax.ppermute(near, 'region', pairs))  1.89 us
  transfers between devices with their start and end apart: 4, of which 3 were waited for; matrix products, arithmetic and copies ran while one was open for 0% of the time, Pallas kernels for 18%

profile of v1, /device:TPU:0, one launch (start us, length us, event | category | flops | bytes accessed | tf_op | source)
XLA Modules:
  0.0 41.7 jit_solution(17432312472291365718)
XLA Ops:
  0.6 3.4 %send.1 = (bf16[432,1024]{1,0:T(8,128)(2,1)}, bf16[432,1024]{1,0:T(8,128)(2,1)}, f32[8,16,512]{2,1,0:T(8,128)}) custom-call(f32[9,35,256]{2,1,0:T(8,128)} %q0_ref.1, f32[9,35,256]{2,1,0:T(8,128)} %q1_ref.1, f32[9,35,256]{2,1,0:T(8,128)} %q2_ref.1, bf16[64,96]{1,0:T(8,128)(2,1)} %constant.2.clone.select_hbm, s32[1,128]{1,0:T(1,128)} %bitcast.6, ...), custom_call_target="tpu_custom_call" | custom-call | flops 268435456 | bytes 3145728 | tf_op jit(solution)/shard_map/send/pallas_call | solution.py:524
  4.0 6.4 %all-to-all-start = ((f32[8,16,512]{2,1,0:T(8,128)}), f32[8,16,512]{2,1,0:T(8,128)S(1)}, u32[]{:S(2)}, u32[]{:S(2)}) async-start(f32[8,16,512]{2,1,0:T(8,128)} %get-tuple-element.19), calls=%async_computation | async-start | bytes 524288 | tf_op jit(solution)/shard_map/all_to_all | solution.py:592
  10.4 5.1 %own.1 = (f32[432,1024]{1,0:T(8,128)S(1)}, f32[9,35,256]{2,1,0:T(8,128)S(1)}, f32[9,35,256]{2,1,0:T(8,128)S(1)}, f32[9,35,256]{2,1,0:T(8,128)S(1)}, bf16[40,192]...) custom-call(f32[9,35,256]{2,1,0:T(8,128)} %q0_ref.1, f32[9,35,256]{2,1,0:T(8,128)} %q1_ref.1, ...), custom_call_target="tpu_custom_call" | custom-call | flops 4294967296 | bytes 8388608 | tf_op jit(solution)/shard_map/own/pallas_call | solution.py:524
  15.5 4.6 %all-to-all-done.got_ref = f32[8,16,512]{2,1,0:T(8,128)S(1)} async-done(((f32[8,16,512]{2,1,0:T(8,128)}), f32[8,16,512]{2,1,0:T(8,128)S(1)}, u32[]{:S(2)}, u32[]{:S(2)}) %all-to-all-start) | async-done | bytes 262176 | tf_op jit(solution)/shard_map/all_to_all | solution.py:592
  20.1 0.1 pick.1.refs_0_
  20.2 2.5 %collective-permute-start = (f32[32,256]{1,0:T(8,128)S(1)}, f32[32,256]{1,0:T(8,128)S(1)}, u32[]{:S(2)}, u32[]{:S(2)}) collective-permute-start(f32[32,256]{1,0:T(8,128)S(1)} %pick.1.refs_0_), channel_id=1, source_target_pairs={{0,24},{8,0},{16,8},{24,16},{1,25},{9,1},{17,9},{25,17},{2,26},{10... | collective-permute-start | bytes 98312 | tf_op jit(solution)/shard_map/ppermute | solution.py:629
  22.7 0.5 %collective-permute-start.1 = (f32[32,256]{1,0:T(8,128)S(1)}, f32[32,256]{1,0:T(8,128)S(1)}, u32[]{:S(2)}, u32[]{:S(2)}) collective-permute-start(f32[32,256]{1,0:T(8,128)S(1)} %pick.1.refs_0_), channel_id=1, source_target_pairs={{0,16},{8,24},{16,0},{24,8},{1,17},{9,25},{17,1},{25,9},{2,18},{10... | collective-permute-start | bytes 98312 | tf_op jit(solution)/shard_map/ppermute | solution.py:629
  23.2 0.6 %collective-permute-start.2 = (f32[32,256]{1,0:T(8,128)S(1)}, f32[32,256]{1,0:T(8,128)S(1)}, u32[]{:S(2)}, u32[]{:S(2)}) collective-permute-start(f32[32,256]{1,0:T(8,128)S(1)} %pick.1.refs_0_), channel_id=1, source_target_pairs={{0,8},{8,16},{16,24},{24,0},{1,9},{9,17},{17,25},{25,1},{2,10},{10... | collective-permute-start | bytes 98312 | tf_op jit(solution)/shard_map/ppermute | solution.py:629
  23.8 2.3 %jump.1 = (f32[9,35,256]{2,1,0:T(8,128)S(1)}, f32[9,35,256]{2,1,0:T(8,128)S(1)}, f32[9,35,256]{2,1,0:T(8,128)S(1)}) custom-call(f32[8,16,512]{2,1,0:T(8,128)S(1)} %all-to-all-done.got_ref, s32[4,256]{1,0:T(4,128)} %neighbor_hbm.1, s32[4,256]{1,0:T(4,128)} %orient_hbm.1, f32[432,1024]{1,0:T(8,128)S(1)} %get-tuple-element.22.own_ref, ...), custom_call_target="tpu_custom_call" | custom-call | flops 2147483648 | bytes 8388608 | tf_op jit(solution)/shard_map/jump/pallas_call | solution.py:524
  26.1 0.0 collective-permute-done.refs_1_
  26.1 0.5 %collective-permute-done.1.refs_2_ = f32[32,256]{1,0:T(8,128)S(1)} collective-permute-done((f32[32,256]{1,0:T(8,128)S(1)}, f32[32,256]{1,0:T(8,128)S(1)}, u32[]{:S(2)}, u32[]{:S(2)}) %collective-permute-start.1) | collective-permute-done | bytes 32800 | tf_op jit(solution)/shard_map/ppermute | solution.py:629
  26.6 1.4 %collective-permute-done.2.refs_3_ = f32[32,256]{1,0:T(8,128)S(1)} collective-permute-done((f32[32,256]{1,0:T(8,128)S(1)}, f32[32,256]{1,0:T(8,128)S(1)}, u32[]{:S(2)}, u32[]{:S(2)}) %collective-permute-start.2) | collective-permute-done | bytes 32800 | tf_op jit(solution)/shard_map/ppermute | solution.py:629
  28.0 0.0 copy-start
  28.0 0.0 copy-start.1
  28.0 2.3 %step.1 = (f32[9,35,256]{2,1,0:T(8,128)}, f32[9,35,256]{2,1,0:T(8,128)}, f32[32,8,128]{2,1,0:T(8,128)S(1)}) custom-call(f32[32,256]{1,0:T(8,128)S(1)} %pick.1.refs_0_, f32[32,256]{1,0:T(8,128)S(1)} %collective-permute-done.refs_1_, f32[32,256]{1,0:T(8,128)S(1)} %collective-permute-done.1.refs_2_, f32[32,256]{1,0:T(8,128)S(1)} %collective-permute-done.2.refs_3_, ...), custom_call_target="tpu_custom_call" | custom-call | flops 1073741824 | bytes 4194304 | tf_op jit(solution)/shard_map/step/pallas_call | solution.py:524
  30.3 10.6 %all_to_all.10.arrived_ref = f32[32,8,128]{2,1,0:T(8,128)S(1)} all-to-all(f32[32,8,128]{2,1,0:T(8,128)S(1)} %get-tuple-element.34), channel_id=1, replica_groups=mesh['region'=4,'wave'=8] {'region','wave'}, dimensions={0} | all-to-all | bytes 262144 | tf_op jit(solution)/shard_map/all_to_all | solution.py:675
  40.9 0.0 copy-done
  40.9 0.0 copy-done.1
  40.9 0.8 %total.1 = f32[30,32]{1,0:T(8,128)} custom-call(f32[32,8,128]{2,1,0:T(8,128)S(1)} %all_to_all.10.arrived_ref, f32[30,32]{1,0:T(8,128)S(1)} %copy-done.1, f32[30,32]{1,0:T(8,128)S(1)} %copy-done), custom_call_target="tpu_custom_call" | custom-call | tf_op jit(solution)/shard_map/total/pallas_call | solution.py:524
Async XLA Ops:
  4.0 16.1 %all-to-all-start = ((f32[8,16,512]{2,1,0:T(8,128)}), f32[8,16,512]{2,1,0:T(8,128)S(1)}, u32[]{:S(2)}, u32[]{:S(2)}) async-start(f32[8,16,512]{2,1,0:T(8,128)} %get-tuple-element.19), calls=%async_computation | async-start | bytes 524288 | tf_op jit(solution)/shard_map/all_to_all | solution.py:592
  20.2 5.9 %collective-permute-start = (f32[32,256]{1,0:T(8,128)S(1)}, f32[32,256]{1,0:T(8,128)S(1)}, u32[]{:S(2)}, u32[]{:S(2)}) collective-permute-start(f32[32,256]{1,0:T(8,128)S(1)} %pick.1.refs_0_), channel_id=1, source_target_pairs={{0,24},{8,0},{16,8},{24,16},{1,25},{9,1},{17,9},{25,17},{2,26},{10... | collective-permute-start | bytes 98312 | tf_op jit(solution)/shard_map/ppermute | solution.py:629
  22.7 3.9 %collective-permute-start.1 = (f32[32,256]{1,0:T(8,128)S(1)}, f32[32,256]{1,0:T(8,128)S(1)}, u32[]{:S(2)}, u32[]{:S(2)}) collective-permute-start(f32[32,256]{1,0:T(8,128)S(1)} %pick.1.refs_0_), channel_id=1, source_target_pairs={{0,16},{8,24},{16,0},{24,8},{1,17},{9,25},{17,1},{25,9},{2,18},{10... | collective-permute-start | bytes 98312 | tf_op jit(solution)/shard_map/ppermute | solution.py:629
  23.2 4.8 %collective-permute-start.2 = (f32[32,256]{1,0:T(8,128)S(1)}, f32[32,256]{1,0:T(8,128)S(1)}, u32[]{:S(2)}, u32[]{:S(2)}) collective-permute-start(f32[32,256]{1,0:T(8,128)S(1)} %pick.1.refs_0_), channel_id=1, source_target_pairs={{0,8},{8,16},{16,24},{24,0},{1,9},{9,17},{17,25},{25,1},{2,10},{10... | collective-permute-start | bytes 98312 | tf_op jit(solution)/shard_map/ppermute | solution.py:629
  28.0 12.9 %copy-start = (f32[30,32]{1,0:T(8,128)S(1)}, f32[30,32]{1,0:T(8,128)}, u32[]{:S(2)}) copy-start(f32[30,32]{1,0:T(8,128)} %coarse_ref.1) | copy-start | bytes 11524
  28.0 12.9 %copy-start.1 = (f32[30,32]{1,0:T(8,128)S(1)}, f32[30,32]{1,0:T(8,128)}, u32[]{:S(2)}) copy-start(f32[30,32]{1,0:T(8,128)} %reg_ref.1) | copy-start | bytes 11524

commit v2 on v1

v2 whole, which is shorter than its diff:
```python
import functools
import jax
import jax.numpy as jnp
import numpy as np
from jax import lax
from jax.experimental import pallas as pl
from jax.experimental.pallas import tpu as pltpu
from jax.sharding import PartitionSpec as P

time_step = 0.2
penalty = 0.5
stress_of = ((0, 5, 4), (5, 1, 3), (4, 3, 2))
voigt_pairs = ((0, 0), (1, 1), (2, 2), (1, 2), (0, 2), (0, 1))
F32 = jnp.float32
BF16 = jnp.bfloat16
NODES, FACE, ROWS, BLOCK = 35, 15, 27 * 16, 30
VROW = 40
KROW = 48


def tables():
    triangle = [(one, two) for one in range(5) for two in range(5 - one)]
    volume_nodes = [
        (one, two, three)
        for one in range(5)
        for two in range(5 - one)
        for three in range(5 - one - two)
    ]
    face_index = np.zeros((15, 4), np.int32)
    for entry, (a, b) in enumerate(triangle):
        for face, key in enumerate([(a, b, 0), (a, 0, b), (0, a, b), (a, b, 4 - a - b)]):
            face_index[entry, face] = volume_nodes.index(key)
    orders = [(0, 1, 2), (1, 2, 0), (2, 0, 1), (0, 2, 1), (2, 1, 0), (1, 0, 2)]
    turning = np.zeros((6, 15), np.int32)
    for orient_id, order in enumerate(orders):
        for entry, (a, b) in enumerate(triangle):
            coords = (a, b, 4 - a - b)
            turning[orient_id, entry] = triangle.index((coords[order[0]], coords[order[1]]))
    return face_index, turning


def split(x):
    high = x.astype(BF16)
    low = (x - high.astype(F32)).astype(BF16)
    return high, low


def dot(a, b):
    return jnp.dot(a, b, preferred_element_type=F32)


def dot_nt(a, b):
    return lax.dot_general(a, b, (((1,), (1,)), ((), ())), preferred_element_type=F32)


def pad_rows(x, rows):
    return jnp.concatenate([x, jnp.zeros((rows - x.shape[0],) + x.shape[1:], x.dtype)], axis=0)


def one_hot(ids, count, start=0):
    rows = lax.broadcasted_iota(jnp.int32, (count, ids.shape[1]), 0) + start
    return jnp.where(rows == ids, 1.0, 0.0).astype(BF16)


def turn_rows(turning, orient_row):
    lanes = orient_row.shape[1]
    rows = lax.broadcasted_iota(jnp.int32, (16, lanes), 0)
    result = rows
    for orient_id in range(1, 6):
        table = jnp.zeros((16, lanes), jnp.int32)
        for m in range(15):
            table = jnp.where(rows == m, int(turning[orient_id, m]), table)
        result = jnp.where(orient_row == orient_id, table, result)
    return result


def rotate(x, index):
    first, second = x[0:8], x[8:16]
    halves = []
    for h in range(2):
        part = index[8 * h : 8 * h + 8]
        inside = part & 7
        a = jnp.take_along_axis(first, inside, axis=0)
        b = jnp.take_along_axis(second, inside, axis=0)
        halves.append(jnp.where(part < 8, a, b))
    return jnp.concatenate(halves, axis=0)


def fetch(pairs, sems):
    copies = []
    for index, (source, target) in enumerate(pairs):
        copy = pltpu.make_async_copy(source, target, sems.at[index])
        copy.start()
        copies.append(copy)
    return copies


def gather_kernel(
    q0_hbm,
    q1_hbm,
    q2_hbm,
    select_hbm,
    send_hbm,
    coarse_hbm,
    sent_ref,
    coarse_ref,
    q_ref,
    select_ref,
    send_ref,
    sems,
):
    elements = q_ref.shape[3]
    sends = sent_ref.shape[1]
    copies = fetch(
        [
            (send_hbm, send_ref),
            (q0_hbm, q_ref.at[0]),
            (q1_hbm, q_ref.at[1]),
            (q2_hbm, q_ref.at[2]),
            (select_hbm, select_ref),
            (coarse_hbm, coarse_ref),
        ],
        sems,
    )
    copies[0].wait()
    face = send_ref[...] // elements
    picked = one_hot(send_ref[...] - face * elements, elements)
    twice = jnp.concatenate([face, face], axis=1)

    def pick_elements(s):
        copies[1 + s].wait()
        pieces = []
        for c in range(9):
            pieces += split(pad_rows(q_ref[s, c], KROW))
        return dot(jnp.concatenate(pieces, axis=0), picked).astype(BF16)

    def pick_faces(s, nodes):
        for c in range(0, 9, 2):
            parts = [nodes[2 * KROW * k : 2 * KROW * (k + 1)] for k in range(c, min(c + 2, 9))]
            every = dot(select_ref[...], jnp.concatenate(parts, axis=1))
            which = twice[:, 0 : every.shape[1]]
            value = every[0:16]
            for f in range(1, 4):
                value = jnp.where(which == f, every[16 * f : 16 * f + 16], value)
            for k in range(len(parts)):
                row = (s * 9 + c + k) * 16
                sent_ref[row : row + 16] = value[:, k * sends : (k + 1) * sends]

    nodes = [pick_elements(0), pick_elements(1)]
    copies[4].wait()
    pick_faces(0, nodes[0])
    nodes.append(pick_elements(2))
    pick_faces(1, nodes[1])
    pick_faces(2, nodes[2])
    copies[5].wait()


def pack_kernel(sent_ref, coarse_ref, out_ref):
    waves = out_ref.shape[0]
    slots = sent_ref.shape[1] // waves
    block, width = coarse_ref.shape
    sent = sent_ref[...].T
    for t in range(4):
        part = sent[:, 128 * t : min(128 * t + 128, ROWS)]
        out_ref[:, t * slots : (t + 1) * slots, 0 : part.shape[1]] = part.reshape(
            waves, slots, part.shape[1]
        )
    pieces = spare(block, slots)
    row = 4 * slots
    if fits(block, slots, width):
        own = pad_rows(coarse_ref[...], pieces * slots)
        for h in range(pieces):
            part = own[h * slots : (h + 1) * slots]
            at = ROWS - 384 + h * width
            for w in range(waves):
                out_ref[w, 3 * slots : 4 * slots, at : at + width] = part
    else:
        padded = pad_rows(coarse_ref[...], 32)
        part = jnp.concatenate([padded[8 * j : 8 * j + 8] for j in range(4)], axis=1)
        for w in range(waves):
            out_ref[w, row : row + 8, 0 : 4 * width] = part


def fits(block, slots, width):
    return spare(block, slots) * width <= 512 - ROWS


def spare(block, slots):
    return -(-block // slots)


def pick_kernel(slots, got_ref, out_ref):
    waves = got_ref.shape[0]
    width = out_ref.shape[1] // waves
    for w in range(waves):
        lanes = slice(w * width, (w + 1) * width)
        if fits(BLOCK, slots, width):
            for h in range(spare(BLOCK, slots)):
                at = ROWS - 384 + h * width
                out_ref[h * slots : (h + 1) * slots, lanes] = got_ref[
                    w, 3 * slots : 4 * slots, at : at + width
                ]
        else:
            part = got_ref[w, 4 * slots : 4 * slots + 8]
            for j in range(4):
                out_ref[8 * j : 8 * j + 8, lanes] = part[:, j * width : (j + 1) * width]


def own_kernel(
    turning,
    regions,
    width,
    q0_ref,
    q1_ref,
    q2_ref,
    model_ref,
    geometry_ref,
    neighbor_ref,
    orient_ref,
    derivative_ref,
    lift_ref,
    prolong_ref,
    select_ref,
    normals_ref,
    scale_ref,
    owner_ref,
    local_ref,
    child_ref,
    own_ref,
    vol0_ref,
    vol1_ref,
    vol2_ref,
    lift_out,
    prolong_out,
    restrict_out,
    index_out,
    place_out,
    child_out,
    send_out,
    model_out,
    half_out,
    normal_out,
    left_ref,
    rows_ref,
    trace_ref,
    high_ref,
    low_ref,
):
    elements = q0_ref.shape[2]
    owner = owner_ref[...]
    waves = place_out.shape[0] // (width * regions)
    away = (owner // waves) ^ lax.axis_index("region")
    place = (away * waves + lax.rem(owner, waves)) * width + local_ref[...]
    place_out[...] = one_hot(place, place_out.shape[0])
    devices = place_out.shape[0] // width
    deep = send_out.shape[0] // devices
    column = jnp.broadcast_to(owner.astype(F32), (128, elements)).T
    earlier = []
    for t in range(elements // 128):
        lanes = slice(128 * t, 128 * t + 128)
        rows = lax.broadcasted_iota(jnp.int32, (elements, 128), 0)
        lane = lax.broadcasted_iota(jnp.int32, (elements, 128), 1) + 128 * t
        same = jnp.where(column == owner[:, lanes].astype(F32), 1, 0)
        same = jnp.where(rows < lane, same, 0)
        earlier.append(jnp.sum(same, axis=0, keepdims=True))
    rank = jnp.concatenate(earlier, axis=1)
    group = rank // deep
    spot = owner * deep + (rank - group * deep)
    for q in range(4):
        send_out[:, q * elements : (q + 1) * elements] = one_hot(
            jnp.where(group == q, spot, -1), devices * deep
        )
    child_out[...] = jnp.where(
        lax.broadcasted_iota(jnp.int32, child_out.shape, 0) == child_ref[...], 1.0, 0.0
    )
    model_out[...] = model_ref[...]
    half = 0.5 * scale_ref[...]
    half_out[...] = half
    for j in range(3):
        normal_out[j] = half * normals_ref[j]
    left_ref[...] = jnp.zeros_like(left_ref)
    for k in range(3):
        high, low = split(derivative_ref[k])
        r = k * VROW
        left_ref[r : r + NODES, 0:NODES] = high.astype(F32)
        left_ref[r : r + NODES, KROW : KROW + NODES] = high.astype(F32)
        left_ref[r : r + NODES, 2 * KROW : 2 * KROW + NODES] = low.astype(F32)
    left = jnp.concatenate([left_ref[...].astype(BF16), select_ref[...]], axis=0)
    rows_ref[...] = jnp.zeros_like(rows_ref)
    for f in range(4):
        rows_ref[16 * f : 16 * f + FACE, 0:NODES] = time_step * lift_ref[:, f, :]
    turned = rows_ref[...].T
    high, low = split(turned[0:VROW, 0:64])
    lift_out[...] = jnp.concatenate([high, high, low], axis=1)
    rows_ref[...] = jnp.zeros_like(rows_ref)
    rows_ref[0:80, 0:NODES] = prolong_ref[...].reshape(80, NODES)
    plain = rows_ref[...]
    high, low = split(plain[0:80, 0:KROW])
    restrict_out[...] = jnp.concatenate([high, high, low], axis=1)
    turned = plain.T
    high, low = split(turned[0:VROW, 0:80])
    prolong_out[...] = jnp.concatenate([high, high, low], axis=1)

    geometry = geometry_ref[...]
    for s, (ref, out) in enumerate(
        ((q0_ref, vol0_ref), (q1_ref, vol1_ref), (q2_ref, vol2_ref))
    ):
        local = []
        for c in range(9):
            high, low = split(pad_rows(ref[c], KROW))
            both = dot(left, jnp.concatenate([high, low, high], axis=0))
            local.append(both)
            row = (s * 9 + c) * 16
            for f in range(4):
                at = 3 * VROW + 16 * f
                lanes = slice(f * elements, (f + 1) * elements)
                trace = both[at : at + 16]
                trace_ref[row : row + 16, lanes] = trace
                high_ref[row : row + 16, lanes], low_ref[row : row + 16, lanes] = split(trace)

        def grad(c, i):
            total = None
            for k in range(3):
                term = geometry[3 * i + k : 3 * i + k + 1] * local[c][k * VROW : k * VROW + VROW]
                total = term if total is None else total + term
            return total[0:NODES]

        terms = []
        for i in range(3):
            terms.append(sum(grad(3 + stress_of[i][j], j) for j in range(3)))
        for i, j in voigt_pairs:
            terms.append(2.0 * grad(i, i) if i == j else grad(j, i) + grad(i, j))
        if s == 0:
            for c in range(9):
                out[c] = time_step * terms[c]
        else:
            trace = (0.5 * model_ref[1]) * (terms[3] + terms[4] + terms[5])
            for c in range(9):
                value = (model_ref[0] if c < 3 else model_ref[2]) * terms[c]
                if 3 <= c < 6:
                    value = value + trace
                out[c] = ref[c] + time_step * value

    for f in range(4):
        lanes = slice(f * elements, (f + 1) * elements)
        picked = one_hot(neighbor_ref[f : f + 1], 4 * elements)
        outer = dot(high_ref[...], picked) + dot(low_ref[...], picked)
        index = turn_rows(turning, orient_ref[f : f + 1])
        index_out[:, lanes] = index
        for cs in range(27):
            r = slice(16 * cs, 16 * cs + 16)
            own_ref[r, lanes] = rotate(outer[r], index) - trace_ref[r, lanes]


def model_terms(first, second, third, terms):
    trace = (0.5 * second) * (terms[3] + terms[4] + terms[5])
    values = []
    for c in range(9):
        value = (first if c < 3 else third) * terms[c]
        values.append(value + trace if 3 <= c < 6 else value)
    return values


def turn_kernel(slots, got_ref, index_ref, neighbor_ref, own_ref, jump_ref):
    elements = own_ref.shape[1] // 4
    sends = got_ref.shape[0] * slots
    received = []
    for t in range(4):
        part = got_ref[:, t * slots : (t + 1) * slots, :].reshape(sends, 128).T
        received.append(part if t < 3 else part[0 : ROWS - 384])
    high, low = split(jnp.concatenate(received, axis=0))
    received = jnp.concatenate([high, low], axis=1)
    for f in range(4):
        lanes = slice(f * elements, (f + 1) * elements)
        picked = one_hot(neighbor_ref[f : f + 1], sends, 4 * elements)
        outer = dot(received, jnp.concatenate([picked, picked], axis=0))
        index = index_ref[:, lanes]
        for cs in range(27):
            r = slice(16 * cs, 16 * cs + 16)
            jump_ref[r, lanes] = own_ref[r, lanes] + rotate(outer[r], index)


def flux_kernel(
    jump_ref,
    lift_ref,
    normal_ref,
    half_ref,
    vol0_ref,
    model_ref,
    base_ref,
    moved_ref,
    backed_ref,
):
    elements = model_ref.shape[2]
    lift = lift_ref[...]

    def lifted(pieces):
        high, low = split(jnp.concatenate(pieces, axis=0))
        return dot(lift, jnp.concatenate([high, low, high], axis=0))[0:NODES]

    scaled = [half_ref[f : f + 1] for f in range(4)]
    normal = [[normal_ref[j, f : f + 1] for j in range(3)] for f in range(4)]

    def flux(s):
        def jump(c, f):
            r = (s * 9 + c) * 16
            return jump_ref[r : r + 16, f * elements : (f + 1) * elements]

        result = []
        for i in range(3):
            result.append(
                lifted(
                    [
                        sum(normal[f][j] * jump(3 + stress_of[i][j], f) for j in range(3))
                        for f in range(4)
                    ]
                )
            )
        for i, j in voigt_pairs:
            if i == j:
                result.append(lifted([(2.0 * normal[f][i]) * jump(i, f) for f in range(4)]))
            else:
                result.append(
                    lifted(
                        [
                            normal[f][i] * jump(j, f) + normal[f][j] * jump(i, f)
                            for f in range(4)
                        ]
                    )
                )
        if s == 0:
            return result, None
        return result, [lifted([scaled[f] * jump(c, f) for f in range(4)]) for c in range(9)]

    terms, _ = flux(0)
    for c in range(9):
        base_ref[c] = vol0_ref[c] + terms[c]
    for s, out in ((1, moved_ref), (2, backed_ref)):
        terms, pen = flux(s)
        values = model_terms(model_ref[0], model_ref[1], model_ref[2], terms)
        for c in range(9):
            out[c] = values[c] + pen[c]


def step_kernel(regions, *refs):
    blocks, refs = refs[:regions], refs[regions:]
    (
    base_ref,
    moved_ref,
    backed_ref,
    prolong_ref,
    restrict_ref,
    place_ref,
    child_ref,
    send_ref,
    local_ref,
    observe_ref,
    vol1_ref,
    vol2_ref,
    delta_ref,
    adjoint_ref,
    message_ref,
    spread_ref,
    ) = refs
    devices = message_ref.shape[0]
    share = blocks[0].shape[1]
    elements = child_ref.shape[1]
    total = None
    for s in range(regions):
        high, low = split(blocks[s][...])
        part = dot(
            jnp.concatenate([high, low], axis=0), place_ref[s * share : (s + 1) * share]
        )
        total = part if total is None else total + part
    fetched = total[0:32] + total[32:64]
    child_hot = child_ref[...]
    prolong = prolong_ref[...]
    step_fine = []
    for p in range(3):
        masked = jnp.concatenate(
            [fetched[10 * p + k : 10 * p + k + 1] * child_hot for k in range(10)], axis=0
        )
        high, low = split(masked)
        step_fine.append(dot(prolong, jnp.concatenate([high, low, high], axis=0))[0:NODES])
    base = [base_ref[c] for c in range(9)]
    pushed = model_terms(step_fine[0], step_fine[1], step_fine[2], base)
    observe = time_step * observe_ref[...]
    ahead = []
    for c in range(9):
        value = (vol1_ref[c] + moved_ref[c]) + pushed[c]
        delta_ref[c] = value
        value = (vol2_ref[c] + backed_ref[c]) + observe * value
        adjoint_ref[c] = value
        ahead.append(value)
    grads = [
        sum(ahead[i] * base[i] for i in range(3)),
        0.5 * ((ahead[3] + ahead[4] + ahead[5]) * (base[3] + base[4] + base[5])),
        sum(ahead[c] * base[c] for c in range(3, 9)),
    ]
    rows = []
    for p in range(3):
        high, low = split(pad_rows(grads[p], KROW))
        parts = dot(restrict_ref[...], jnp.concatenate([high, low, high], axis=0))
        for k in range(10):
            rows.append(
                jnp.sum(parts[8 * k : 8 * k + 8] * child_hot, axis=0, keepdims=True)
            )
    rows.append(local_ref[...].astype(F32))
    high, low = split(pad_rows(jnp.concatenate(rows, axis=0), 32))
    spread_ref[...] = jnp.zeros_like(spread_ref)
    for q in range(4):
        lanes = slice(q * elements, (q + 1) * elements)
        spread_ref[0, 32 * q : 32 * q + 32, lanes] = high
        spread_ref[1, 32 * q : 32 * q + 32, lanes] = low
    sends = send_ref[...]
    packed = dot_nt(sends, spread_ref[0]) + dot_nt(sends, spread_ref[1])
    deep = message_ref.shape[1]
    for d in range(devices):
        message_ref[d] = packed[deep * d : deep * d + deep]


def sum_kernel(
    arrived_ref, reg_ref, coarse_ref, delta_ref, adjoint_ref, out_hbm, delta_hbm, adjoint_hbm, out_ref, sems
):
    copies = fetch([(delta_ref, delta_hbm), (adjoint_ref, adjoint_hbm)], sems.at[pl.ds(0, 2)])
    block, width = coarse_ref.shape
    count, deep, _ = arrived_ref.shape
    values = arrived_ref[...].reshape(count * deep, 128)
    lane = lax.broadcasted_iota(jnp.int32, values.shape, 1)
    local = jnp.concatenate(
        [
            jnp.take_along_axis(
                values[r : r + 8], (lane[0:8] & 96) + block, axis=1
            )
            for r in range(0, count * deep, 8)
        ],
        axis=0,
    )
    hot = jnp.where(local == (lane & 31).astype(F32), 1.0, 0.0).astype(BF16)
    high, low = split(values)
    table = lax.dot_general(
        jnp.concatenate([high, low], axis=0),
        jnp.concatenate([hot, hot], axis=0),
        (((0,), (0,)), ((), ())),
        preferred_element_type=F32,
    )
    total = sum(table[32 * q : 32 * q + 32, 32 * q : 32 * q + 32] for q in range(4))
    weighted = reg_ref[...] * coarse_ref[...]
    out_ref[...] = total[0:block, 0:width] + weighted
    copies += fetch([(out_ref, out_hbm)], sems.at[pl.ds(2, 1)])
    for copy in copies:
        copy.wait()


HBM, VMEM = pltpu.MemorySpace.HBM, pltpu.MemorySpace.VMEM


def call(kernel, name, ins, outs, scratch=(), limit=16 << 20, flops=0, bytes_accessed=0):
    specs = {
        "h": pl.BlockSpec(memory_space=HBM),
        "v": pl.BlockSpec(memory_space=VMEM),
        "w": pl.BlockSpec(),
        "x": pl.BlockSpec(),
    }
    shapes = []
    for how, shape, dtype in outs:
        if how in "hx":
            shapes.append(HBM(shape, dtype))
        elif how == "v":
            shapes.append(VMEM(shape, dtype))
        else:
            shapes.append(jax.ShapeDtypeStruct(shape, dtype))
    run = pl.pallas_call(
        kernel,
        out_shape=tuple(shapes),
        in_specs=[specs[how] for how in ins],
        out_specs=tuple(specs[how] for how, _, _ in outs),
        scratch_shapes=list(scratch),
        name=name,
        cost_estimate=pl.CostEstimate(
            flops=flops, bytes_accessed=bytes_accessed, transcendentals=0
        ),
        compiler_params=pltpu.CompilerParams(vmem_limit_bytes=limit),
    )

    def placed(*operands):
        fixed = [
            pltpu.with_memory_space_constraint(x, VMEM if how == "v" else HBM)
            for how, x in zip(ins, operands, strict=True)
        ]
        return run(*fixed)

    return placed


def body(
    state0,
    delta,
    adjoint,
    model,
    geometry,
    normals,
    face_scale,
    derivative,
    lift,
    prolong,
    coarse_step,
    reg_weight,
    observe,
    owner,
    coarse_local,
    child,
    neighbor,
    orient,
    send_face,
):
    face_index, turning = tables()
    elements = state0.shape[2]
    wave_size = lax.axis_size("wave")
    devices = lax.axis_size(("region", "wave"))
    sends = send_face.shape[0]
    block, width = coarse_step.shape
    deep = 2 * elements // devices // 4
    everyone = ("region", "wave")
    select = np.zeros((64, 2 * KROW), np.float32)
    for f in range(4):
        for m in range(FACE):
            select[16 * f + m, face_index[m, f]] = 1.0
            select[16 * f + m, KROW + face_index[m, f]] = 1.0
    slots = sends // wave_size
    regions = devices // wave_size
    rows = 4 * slots + 8 * (1 - fits(block, slots, width))
    faces = 4 * elements
    state = (9, NODES, elements)

    sent, mine = call(
        gather_kernel,
        "gather",
        "hhhhhh",
        (("v", (ROWS, sends), F32), ("v", (block, width), F32)),
        scratch=(
            pltpu.VMEM((3, *state), F32),
            pltpu.VMEM(select.shape, BF16),
            pltpu.VMEM((1, sends), jnp.int32),
            pltpu.SemaphoreType.DMA((6,)),
        ),
        bytes_accessed=2 << 20,
        flops=1 << 28,
    )(
        state0,
        delta,
        adjoint,
        jnp.asarray(select, BF16),
        send_face.reshape(1, sends),
        coarse_step,
    )
    (message,) = call(
        pack_kernel, "pack", "vv", (("w", (wave_size, rows, 128), F32),), limit=4 << 20
    )(sent, mine)
    got = lax.all_to_all(message, "wave", split_axis=0, concat_axis=0, tiled=True)
    own, vol0, vol1, vol2, lift_left, prolong_left, restrict_left, index, place, kind, places, speeds, half, normal = call(
        functools.partial(own_kernel, turning, regions, width),
        "own",
        "w" * 16,
        (
            ("v", (ROWS, faces), F32),
            ("v", state, F32),
            ("x", state, F32),
            ("x", state, F32),
            ("v", (VROW, 192), BF16),
            ("v", (VROW, 240), BF16),
            ("v", (80, 3 * KROW), BF16),
            ("v", (16, faces), jnp.int32),
            ("v", (devices * width, elements), BF16),
            ("v", (8, elements), F32),
            ("v", (devices * deep, 4 * elements), BF16),
            ("v", (3, NODES, elements), F32),
            ("v", (4, elements), F32),
            ("v", (3, 4, elements), F32),
        ),
        scratch=(
            pltpu.VMEM((3 * VROW, 3 * KROW), F32),
            pltpu.VMEM((128, 128), F32),
            pltpu.VMEM((ROWS, faces), F32),
            pltpu.VMEM((ROWS, faces), BF16),
            pltpu.VMEM((ROWS, faces), BF16),
        ),
        limit=32 << 20,
        bytes_accessed=8 << 20,
        flops=1 << 32,
    )(
        state0,
        delta,
        adjoint,
        model,
        geometry,
        neighbor,
        orient,
        derivative,
        lift.transpose(2, 0, 1),
        prolong.transpose(2, 0, 1),
        jnp.asarray(np.pad(select, ((0, 0), (0, KROW))), BF16),
        normals,
        face_scale,
        owner.reshape(1, elements),
        coarse_local.reshape(1, elements),
        child.reshape(1, elements),
    )
    share = wave_size * width
    (near,) = call(
        functools.partial(pick_kernel, slots), "pick", "v", (("v", (32, share), F32),), limit=4 << 20
    )(got)
    blocks = [near] + [None] * (regions - 1)
    for s in reversed(range(1, regions)):
        blocks[s] = lax.ppermute(near, "region", [(i, i ^ s) for i in range(regions)])
    (jump,) = call(
        functools.partial(turn_kernel, slots),
        "turn",
        "vvvv",
        (("v", (ROWS, faces), F32),),
        bytes_accessed=2 << 20,
        flops=1 << 29,
    )(got, index, neighbor, own)
    base, moved, backed = call(
        flux_kernel,
        "flux",
        "vvvvvv",
        (("v", state, F32),) * 3,
        bytes_accessed=4 << 20,
        flops=1 << 30,
    )(jump, lift_left, normal, half, vol0, speeds)
    delta_next, adjoint_next, message = call(
        functools.partial(step_kernel, regions),
        "step",
        "v" * (regions + 12),
        (("v", state, F32), ("v", state, F32), ("v", (devices, deep, 128), F32)),
        scratch=(pltpu.VMEM((2, 128, 4 * elements), BF16),),
        limit=12 << 20,
        bytes_accessed=4 << 20,
        flops=1 << 30,
    )(*blocks, base, moved, backed, prolong_left, restrict_left, place, kind, places, coarse_local.reshape(1, elements), observe, vol1, vol2)
    arrived = lax.all_to_all(message, everyone, split_axis=0, concat_axis=0, tiled=True)
    hess_vec, delta_next, adjoint_next = call(
        sum_kernel,
        "total",
        "vvvvv",
        (("h", (block, width), F32), ("h", state, F32), ("h", state, F32)),
        scratch=(pltpu.VMEM((block, width), F32), pltpu.SemaphoreType.DMA((3,))),
        limit=4 << 20,
    )(arrived, reg_weight, coarse_step, delta_next, adjoint_next)
    return (delta_next, adjoint_next, hess_vec)


def solution(mesh):
    both = ("region", "wave")
    wide, flat = P(None, None, both), P(None, both)
    placed = (
        wide,
        wide,
        wide,
        wide,
        flat,
        wide,
        flat,
        P(),
        P(),
        P(),
        flat,
        flat,
        flat,
        P(both, None),
        P(both),
        P(both),
        flat,
        flat,
        P(both),
    )
    return jax.shard_map(
        body, mesh=mesh, in_specs=placed, out_specs=(wide, wide, flat), check_vma=False
    )
```

time: 42 us -> 39.5 us (0.940)
  Pallas kernels: 14 us -> 12.1 us
  blocking collectives: 10.6 us -> 9.08 us
  waiting for transfers between devices: 6.46 us -> 7.32 us
    pallas_call x6 -> x8, Pallas kernels: 14 us -> 12.1 us  [placed(): return run(*fixed)]
    all_to_all x1, blocking collectives: 10.6 us -> 9.08 us  [body(): lax.all_to_all(message, everyone, split_axis=0, concat_axis=0, tiled=True)]
    ppermute x3, waiting for transfers between devices: 1.89 us -> 2.65 us  [body(): lax.ppermute(near, 'region', [(i, i ^ s) for i in range(regions)])]
  transfers between devices with their start and end apart: 4 -> 4, of which waited for: 3 -> 3; matrix products, arithmetic and copies ran while one was open for 0% -> 0% of each run, Pallas kernels for 18% -> 17%
where the time goes in v2:
time: 39.5 us; the launch traced here: 39.2 us
  Pallas kernels  12.1 us (31%)
  starting transfers between devices  9.91 us (25%)
  blocking collectives  9.08 us (23%)
  waiting for transfers between devices  7.32 us (19%)
  between operations  0.75 us (2%)
    pallas_call x8, Pallas kernels, placed(): return run(*fixed)  12.1 us
    all_to_all x1, blocking collectives, body(): lax.all_to_all(message, everyone, split_axis=0, concat_axis=0, tiled=True)  9.08 us
    all_to_all x1, starting transfers between devices, body(): lax.all_to_all(message, 'wave', split_axis=0, concat_axis=0, tiled=True)  6.35 us
    all_to_all x1, waiting for transfers between devices, body(): lax.all_to_all(message, 'wave', split_axis=0, concat_axis=0, tiled=True)  4.66 us
    ppermute x3, starting transfers between devices, body(): lax.ppermute(near, 'region', [(i, i ^ s) for i in range(regions)])  3.55 us
    ppermute x3, waiting for transfers between devices, body(): lax.ppermute(near, 'region', [(i, i ^ s) for i in range(regions)])  2.65 us
  transfers between devices with their start and end apart: 4, of which 3 were waited for; matrix products, arithmetic and copies ran while one was open for 0% of the time, Pallas kernels for 17%

profile of v2, /device:TPU:0, one launch (start us, length us, event | category | flops | bytes accessed | tf_op | source)
XLA Modules:
  0.0 39.2 jit_solution(17528228179218134346)
XLA Ops:
  0.6 2.5 %gather.1 = (f32[432,128]{1,0:T(8,128)S(1)}, f32[30,32]{1,0:T(8,128)S(1)}) custom-call(f32[9,35,256]{2,1,0:T(8,128)} %q0_ref.1, f32[9,35,256]{2,1,0:T(8,128)} %q1_ref.1, f32[9,35,256]{2,1,0:T(8,128)} %q2_ref.1, bf16[64,96]{1,0:T(8,128)(2,1)} %constant.4.clone.select_hbm, s32[1,128]{1,0:T(1,128)} %bitcast.8, f32[30,32]{1,0:T(8,128)} %coarse_ref.1), custom_call_target="tpu_custom_call" | custom-call | flops 268435456 | bytes 2097152 | tf_op jit(solution)/shard_map/gather/pallas_call | solution.py:591
  3.1 0.9 %pack.1 = f32[8,64,128]{2,1,0:T(8,128)} custom-call(f32[432,128]{1,0:T(8,128)S(1)} %get-tuple-element.28.sent_ref, f32[30,32]{1,0:T(8,128)S(1)} %get-tuple-element.29.coarse_ref), custom_call_target="tpu_custom_call" | custom-call | tf_op jit(solution)/shard_map/pack/pallas_call | solution.py:591
  4.0 6.4 %all-to-all-start = ((f32[8,64,128]{2,1,0:T(8,128)}), f32[8,64,128]{2,1,0:T(8,128)S(1)}, u32[]{:S(2)}, u32[]{:S(2)}) async-start(f32[8,64,128]{2,1,0:T(8,128)} %pack.1), calls=%async_computation | async-start | bytes 524288 | tf_op jit(solution)/shard_map/all_to_all | solution.py:660
  10.3 0.0 copy-start.2
  10.3 5.0 %own.1 = (f32[432,1024]{1,0:T(8,128)S(1)}, f32[9,35,256]{2,1,0:T(8,128)S(1)}, f32[9,35,256]{2,1,0:T(8,128)}, f32[9,35,256]{2,1,0:T(8,128)}, bf16[40,192]{1,0:T(8...) custom-call(f32[9,35,256]{2,1,0:T(8,128)} %q0_ref.1, ...), custom_call_target="tpu_custom_call" | custom-call | flops 4294967296 | bytes 8388608 | tf_op jit(solution)/shard_map/own/pallas_call | solution.py:591
  15.4 4.7 %all-to-all-done.got_ref = f32[8,64,128]{2,1,0:T(8,128)S(1)} async-done(((f32[8,64,128]{2,1,0:T(8,128)}), f32[8,64,128]{2,1,0:T(8,128)S(1)}, u32[]{:S(2)}, u32[]{:S(2)}) %all-to-all-start) | async-done | bytes 262176 | tf_op jit(solution)/shard_map/all_to_all | solution.py:660
  20.0 0.1 pick.1.refs_0_
  20.1 1.6 %collective-permute-start = (f32[32,256]{1,0:T(8,128)S(1)}, f32[32,256]{1,0:T(8,128)S(1)}, u32[]{:S(2)}, u32[]{:S(2)}) collective-permute-start(f32[32,256]{1,0:T(8,128)S(1)} %pick.1.refs_0_), channel_id=1, source_target_pairs={{0,8},{8,0},{16,24},{24,16},{1,9},{9,1},{17,25},{25,17},{2,10},{10... | collective-permute-start | bytes 98312 | tf_op jit(solution)/shard_map/ppermute | solution.py:715
  21.7 1.5 %collective-permute-start.1 = (f32[32,256]{1,0:T(8,128)S(1)}, f32[32,256]{1,0:T(8,128)S(1)}, u32[]{:S(2)}, u32[]{:S(2)}) collective-permute-start(f32[32,256]{1,0:T(8,128)S(1)} %pick.1.refs_0_), channel_id=1, source_target_pairs={{0,16},{8,24},{16,0},{24,8},{1,17},{9,25},{17,1},{25,9},{2,18},{10... | collective-permute-start | bytes 98312 | tf_op jit(solution)/shard_map/ppermute | solution.py:715
  23.2 0.5 %collective-permute-start.2 = (f32[32,256]{1,0:T(8,128)S(1)}, f32[32,256]{1,0:T(8,128)S(1)}, u32[]{:S(2)}, u32[]{:S(2)}) collective-permute-start(f32[32,256]{1,0:T(8,128)S(1)} %pick.1.refs_0_), channel_id=1, source_target_pairs={{0,24},{8,16},{16,8},{24,0},{1,25},{9,17},{17,9},{25,1},{2,26},{10... | collective-permute-start | bytes 98312 | tf_op jit(solution)/shard_map/ppermute | solution.py:715
  23.7 0.0 copy-done.2
  23.7 0.5 %turn.1.jump_ref = f32[432,1024]{1,0:T(8,128)S(1)} custom-call(f32[8,64,128]{2,1,0:T(8,128)S(1)} %all-to-all-done.got_ref, s32[16,1024]{1,0:T(8,128)S(1)} %get-tuple-element.30.index_ref, s32[4,256]{1,0:T(4,128)S(1)} %copy-done.2, f32[432,1024]{1,0:T(8,128)S(1)} %get-tuple-element.31.own_ref), custom_call_target="tpu_custom_call" | custom-call | flops 536870912 | bytes 2097152 | tf_op jit(solution)/shard_map/turn/pallas_call | solution.py:591
  24.2 0.0 copy-start.3
  24.2 0.0 copy-start.4
  24.2 0.0 copy-start.5
  24.2 0.0 copy-start.6
  24.2 1.1 %flux.1 = (f32[9,35,256]{2,1,0:T(8,128)S(1)}, f32[9,35,256]{2,1,0:T(8,128)S(1)}, f32[9,35,256]{2,1,0:T(8,128)S(1)}) custom-call(f32[432,1024]{1,0:T(8,128)S(1)} %turn.1.jump_ref, bf16[40,192]{1,0:T(8,128)(2,1)S(1)} %get-tuple-element.32.lift_ref, f32[3,4,256]{2,1,0:T(4,128)S(1)} %get-tuple-element.33.normal_ref, f32[4,256]{1,0:T(4,128)S(1)} %get-tuple-element.34.half_ref, ...), custom_call_target="tpu_custom_call" | custom-call | flops 1073741824 | bytes 4194304 | tf_op jit(solution)/shard_map/flux/pallas_call | solution.py:591
  25.3 0.0 collective-permute-done.refs_1_
  25.4 0.2 collective-permute-done.1.refs_2_
  25.6 2.4 %collective-permute-done.2.refs_3_ = f32[32,256]{1,0:T(8,128)S(1)} collective-permute-done((f32[32,256]{1,0:T(8,128)S(1)}, f32[32,256]{1,0:T(8,128)S(1)}, u32[]{:S(2)}, u32[]{:S(2)}) %collective-permute-start.2) | collective-permute-done | bytes 32800 | tf_op jit(solution)/shard_map/ppermute | solution.py:715
  28.0 0.0 copy-done.3
  28.0 0.0 copy-done.4
  28.0 0.0 copy-done.5
  28.0 0.0 copy-done.6
  28.0 0.0 copy-start
  28.0 0.0 copy-start.1
  28.1 1.1 %step.1 = (f32[9,35,256]{2,1,0:T(8,128)S(1)}, f32[9,35,256]{2,1,0:T(8,128)S(1)}, f32[32,4,128]{2,1,0:T(4,128)S(1)}) custom-call(f32[32,256]{1,0:T(8,128)S(1)} %pick.1.refs_0_, f32[32,256]{1,0:T(8,128)S(1)} %collective-permute-done.refs_1_, f32[32,256]{1,0:T(8,128)S(1)} %collective-permute-done.1.refs_2_, f32[32,256]{1,0:T(8,128)S(1)} %collective-permute-done.2.refs_3_, ...), custom_call_target="tpu_custom_call" | custom-call | flops 1073741824 | bytes 4194304 | tf_op jit(solution)/shard_map/step/pallas_call | solution.py:591
  29.2 9.1 %all_to_all.10.arrived_ref = f32[32,4,128]{2,1,0:T(4,128)S(1)} all-to-all(f32[32,4,128]{2,1,0:T(4,128)S(1)} %get-tuple-element.47), channel_id=1, replica_groups=mesh['region'=4,'wave'=8] {'region','wave'}, dimensions={0} | all-to-all | bytes 131072 | tf_op jit(solution)/shard_map/all_to_all | solution.py:742
  38.2 0.0 copy-done
  38.2 0.0 copy-done.1
  38.2 0.9 %total.1 = (f32[30,32]{1,0:T(8,128)}, f32[9,35,256]{2,1,0:T(8,128)}, f32[9,35,256]{2,1,0:T(8,128)}) custom-call(f32[32,4,128]{2,1,0:T(4,128)S(1)} %all_to_all.10.arrived_ref, f32[30,32]{1,0:T(8,128)S(1)} %copy-done.1, f32[30,32]{1,0:T(8,128)S(1)} %copy-done, f32[9,35,256]{2,1,0:T(8,128)S(1)} %get-tuple-element.48.delta_ref, ...), custom_call_target="tpu_custom_call" | custom-call | tf_op jit(solution)/shard_map/total/pallas_call | solution.py:591
Async XLA Ops:
  4.0 16.1 %all-to-all-start = ((f32[8,64,128]{2,1,0:T(8,128)}), f32[8,64,128]{2,1,0:T(8,128)S(1)}, u32[]{:S(2)}, u32[]{:S(2)}) async-start(f32[8,64,128]{2,1,0:T(8,128)} %pack.1), calls=%async_computation | async-start | bytes 524288 | tf_op jit(solution)/shard_map/all_to_all | solution.py:660
  10.3 13.4 %copy-start.2 = (s32[4,256]{1,0:T(4,128)S(1)}, s32[4,256]{1,0:T(4,128)}, u32[]{:S(2)}) copy-start(s32[4,256]{1,0:T(4,128)} %neighbor_ref.3) | copy-start | bytes 12292
  20.1 5.2 %collective-permute-start = (f32[32,256]{1,0:T(8,128)S(1)}, f32[32,256]{1,0:T(8,128)S(1)}, u32[]{:S(2)}, u32[]{:S(2)}) collective-permute-start(f32[32,256]{1,0:T(8,128)S(1)} %pick.1.refs_0_), channel_id=1, source_target_pairs={{0,8},{8,0},{16,24},{24,16},{1,9},{9,1},{17,25},{25,17},{2,10},{10... | collective-permute-start | bytes 98312 | tf_op jit(solution)/shard_map/ppermute | solution.py:715
  21.7 3.9 %collective-permute-start.1 = (f32[32,256]{1,0:T(8,128)S(1)}, f32[32,256]{1,0:T(8,128)S(1)}, u32[]{:S(2)}, u32[]{:S(2)}) collective-permute-start(f32[32,256]{1,0:T(8,128)S(1)} %pick.1.refs_0_), channel_id=1, source_target_pairs={{0,16},{8,24},{16,0},{24,8},{1,17},{9,25},{17,1},{25,9},{2,18},{10... | collective-permute-start | bytes 98312 | tf_op jit(solution)/shard_map/ppermute | solution.py:715
  23.2 4.8 %collective-permute-start.2 = (f32[32,256]{1,0:T(8,128)S(1)}, f32[32,256]{1,0:T(8,128)S(1)}, u32[]{:S(2)}, u32[]{:S(2)}) collective-permute-start(f32[32,256]{1,0:T(8,128)S(1)} %pick.1.refs_0_), channel_id=1, source_target_pairs={{0,24},{8,16},{16,8},{24,0},{1,25},{9,17},{17,9},{25,1},{2,26},{10... | collective-permute-start | bytes 98312 | tf_op jit(solution)/shard_map/ppermute | solution.py:715
  24.2 3.9 %copy-start.3 = (f32[35,256]{1,0:T(8,128)S(1)}, f32[35,256]{1,0:T(8,128)}, u32[]{:S(2)}) copy-start(f32[35,256]{1,0:T(8,128)} %refs_13_.1) | copy-start | bytes 107524
  24.2 3.8 %copy-start.4 = (s32[256]{0:T(256)S(1)}, s32[256]{0:T(256)}, u32[]{:S(2)}) copy-start(s32[256]{0:T(256)} %param.35) | copy-start | bytes 3076
  24.2 3.8 %copy-start.5 = (f32[9,35,256]{2,1,0:T(8,128)S(1)}, f32[9,35,256]{2,1,0:T(8,128)}, u32[]{:S(2)}) copy-start(f32[9,35,256]{2,1,0:T(8,128)} %get-tuple-element.45.refs_14_) | copy-start | bytes 967684
  24.2 3.8 %copy-start.6 = (f32[9,35,256]{2,1,0:T(8,128)S(1)}, f32[9,35,256]{2,1,0:T(8,128)}, u32[]{:S(2)}) copy-start(f32[9,35,256]{2,1,0:T(8,128)} %get-tuple-element.46.refs_15_) | copy-start | bytes 967684
  28.0 10.2 %copy-start = (f32[30,32]{1,0:T(8,128)S(1)}, f32[30,32]{1,0:T(8,128)}, u32[]{:S(2)}) copy-start(f32[30,32]{1,0:T(8,128)} %coarse_ref.1) | copy-start | bytes 11524
  28.0 10.2 %copy-start.1 = (f32[30,32]{1,0:T(8,128)S(1)}, f32[30,32]{1,0:T(8,128)}, u32[]{:S(2)}) copy-start(f32[30,32]{1,0:T(8,128)} %reg_ref.1) | copy-start | bytes 11524

commit v3 on v2

--- a/solution.py
+++ b/solution.py
@@ -7,8 +7,8 @@
 from jax.experimental.pallas import tpu as pltpu
 from jax.sharding import PartitionSpec as P
 
+
 time_step = 0.2
-penalty = 0.5
 stress_of = ((0, 5, 4), (5, 1, 3), (4, 3, 2))
 voigt_pairs = ((0, 0), (1, 1), (2, 2), (1, 2), (0, 2), (0, 1))
 F32 = jnp.float32
@@ -96,28 +96,26 @@
 
 
 def gather_kernel(
+    face_index,
     q0_hbm,
     q1_hbm,
     q2_hbm,
-    select_hbm,
     send_hbm,
     coarse_hbm,
-    sent_ref,
+    out_ref,
+    q_ref,
+    send_ref,
     coarse_ref,
-    q_ref,
-    select_ref,
-    send_ref,
     sems,
 ):
     elements = q_ref.shape[3]
-    sends = sent_ref.shape[1]
+    sends = send_ref.shape[1]
     copies = fetch(
         [
             (send_hbm, send_ref),
             (q0_hbm, q_ref.at[0]),
             (q1_hbm, q_ref.at[1]),
             (q2_hbm, q_ref.at[2]),
-            (select_hbm, select_ref),
             (coarse_hbm, coarse_ref),
         ],
         sems,
@@ -125,41 +123,33 @@
     copies[0].wait()
     face = send_ref[...] // elements
     picked = one_hot(send_ref[...] - face * elements, elements)
-    twice = jnp.concatenate([face, face], axis=1)
-
-    def pick_elements(s):
-        copies[1 + s].wait()
-        pieces = []
-        for c in range(9):
-            pieces += split(pad_rows(q_ref[s, c], KROW))
-        return dot(jnp.concatenate(pieces, axis=0), picked).astype(BF16)
-
-    def pick_faces(s, nodes):
-        for c in range(0, 9, 2):
-            parts = [nodes[2 * KROW * k : 2 * KROW * (k + 1)] for k in range(c, min(c + 2, 9))]
-            every = dot(select_ref[...], jnp.concatenate(parts, axis=1))
-            which = twice[:, 0 : every.shape[1]]
-            value = every[0:16]
-            for f in range(1, 4):
-                value = jnp.where(which == f, every[16 * f : 16 * f + 16], value)
-            for k in range(len(parts)):
-                row = (s * 9 + c + k) * 16
-                sent_ref[row : row + 16] = value[:, k * sends : (k + 1) * sends]
-
-    nodes = [pick_elements(0), pick_elements(1)]
-    copies[4].wait()
-    pick_faces(0, nodes[0])
-    nodes.append(pick_elements(2))
-    pick_faces(1, nodes[1])
-    pick_faces(2, nodes[2])
-    copies[5].wait()
-
-
-def pack_kernel(sent_ref, coarse_ref, out_ref):
+    rows = lax.broadcasted_iota(jnp.int32, (16, sends), 0)
+    index = jnp.zeros((16, sends), jnp.int32)
+    for f in range(4):
+        table = jnp.zeros((16, sends), jnp.int32)
+        for m in range(FACE):
+            table = jnp.where(rows == m, int(face_index[m, f]), table)
+        index = jnp.where(face == f, table, index)
+    inside, tile = index & 7, index >> 3
+    for copy in copies[1:]:
+        copy.wait()
+    fields = [pad_rows(q_ref[s, c], VROW) for s in range(3) for c in range(9)]
+    high, low = split(pad_rows(jnp.concatenate(fields, axis=0), len(fields) * VROW + 8))
+    count = high.shape[0]
+    nodes = dot(jnp.concatenate([high, low], axis=0), picked)
+    traces = []
+    for at in range(0, len(fields) * VROW, VROW):
+        both = nodes[at : at + VROW] + nodes[count + at : count + at + VROW]
+        for h in range(0, 16, 8):
+            value = None
+            for t in range(VROW // 8):
+                part = jnp.take_along_axis(both[8 * t : 8 * t + 8], inside[h : h + 8], axis=0)
+                value = part if t == 0 else jnp.where(tile[h : h + 8] == t, part, value)
+            traces.append(value)
     waves = out_ref.shape[0]
-    slots = sent_ref.shape[1] // waves
+    slots = sends // waves
     block, width = coarse_ref.shape
-    sent = sent_ref[...].T
+    sent = jnp.concatenate(traces, axis=0).T
     for t in range(4):
         part = sent[:, 128 * t : min(128 * t + 128, ROWS)]
         out_ref[:, t * slots : (t + 1) * slots, 0 : part.shape[1]] = part.reshape(
@@ -555,7 +545,7 @@
 HBM, VMEM = pltpu.MemorySpace.HBM, pltpu.MemorySpace.VMEM
 
 
-def call(kernel, name, ins, outs, scratch=(), limit=16 << 20, flops=0, bytes_accessed=0):
+def call(kernel, ins, outs, scratch=(), limit=16 << 20, flops=0, bytes_accessed=0):
     specs = {
         "h": pl.BlockSpec(memory_space=HBM),
         "v": pl.BlockSpec(memory_space=VMEM),
@@ -576,7 +566,6 @@
         in_specs=[specs[how] for how in ins],
         out_specs=tuple(specs[how] for how, _, _ in outs),
         scratch_shapes=list(scratch),
-        name=name,
         cost_estimate=pl.CostEstimate(
             flops=flops, bytes_accessed=bytes_accessed, transcendentals=0
         ),
@@ -633,34 +622,22 @@
     faces = 4 * elements
     state = (9, NODES, elements)
 
-    sent, mine = call(
-        gather_kernel,
-        "gather",
-        "hhhhhh",
-        (("v", (ROWS, sends), F32), ("v", (block, width), F32)),
+    (message,) = call(
+        functools.partial(gather_kernel, face_index),
+        "hhhhh",
+        (("w", (wave_size, rows, 128), F32),),
         scratch=(
             pltpu.VMEM((3, *state), F32),
-            pltpu.VMEM(select.shape, BF16),
             pltpu.VMEM((1, sends), jnp.int32),
-            pltpu.SemaphoreType.DMA((6,)),
+            pltpu.VMEM((block, width), F32),
+            pltpu.SemaphoreType.DMA((5,)),
         ),
         bytes_accessed=2 << 20,
         flops=1 << 28,
-    )(
-        state0,
-        delta,
-        adjoint,
-        jnp.asarray(select, BF16),
-        send_face.reshape(1, sends),
-        coarse_step,
-    )
-    (message,) = call(
-        pack_kernel, "pack", "vv", (("w", (wave_size, rows, 128), F32),), limit=4 << 20
-    )(sent, mine)
+    )(state0, delta, adjoint, send_face.reshape(1, sends), coarse_step)
     got = lax.all_to_all(message, "wave", split_axis=0, concat_axis=0, tiled=True)
     own, vol0, vol1, vol2, lift_left, prolong_left, restrict_left, index, place, kind, places, speeds, half, normal = call(
         functools.partial(own_kernel, turning, regions, width),
-        "own",
         "w" * 16,
         (
             ("v", (ROWS, faces), F32),
@@ -708,30 +685,23 @@
     )
     share = wave_size * width
     (near,) = call(
-        functools.partial(pick_kernel, slots), "pick", "v", (("v", (32, share), F32),), limit=4 << 20
+        functools.partial(pick_kernel, slots), "v", (("v", (32, share), F32),), limit=4 << 20
     )(got)
     blocks = [near] + [None] * (regions - 1)
     for s in reversed(range(1, regions)):
         blocks[s] = lax.ppermute(near, "region", [(i, i ^ s) for i in range(regions)])
     (jump,) = call(
         functools.partial(turn_kernel, slots),
-        "turn",
         "vvvv",
         (("v", (ROWS, faces), F32),),
         bytes_accessed=2 << 20,
         flops=1 << 29,
     )(got, index, neighbor, own)
     base, moved, backed = call(
-        flux_kernel,
-        "flux",
-        "vvvvvv",
-        (("v", state, F32),) * 3,
-        bytes_accessed=4 << 20,
-        flops=1 << 30,
+        flux_kernel, "vvvvvv", (("v", state, F32),) * 3, bytes_accessed=4 << 20, flops=1 << 30
     )(jump, lift_left, normal, half, vol0, speeds)
     delta_next, adjoint_next, message = call(
         functools.partial(step_kernel, regions),
-        "step",
         "v" * (regions + 12),
         (("v", state, F32), ("v", state, F32), ("v", (devices, deep, 128), F32)),
         scratch=(pltpu.VMEM((2, 128, 4 * elements), BF16),),
@@ -742,7 +712,6 @@
     arrived = lax.all_to_all(message, everyone, split_axis=0, concat_axis=0, tiled=True)
     hess_vec, delta_next, adjoint_next = call(
         sum_kernel,
-        "total",
         "vvvvv",
         (("h", (block, width), F32), ("h", state, F32), ("h", state, F32)),
         scratch=(pltpu.VMEM((block, width), F32), pltpu.SemaphoreType.DMA((3,))),

time: 39.5 us -> 38.7 us (0.980)
  Pallas kernels: 12.1 us -> 11.3 us
    pallas_call x8 -> x7, Pallas kernels: 12.1 us -> 11.3 us  [placed(): return run(*fixed)]
where the time goes in v3:
time: 38.7 us; the launch traced here: 38.4 us
  Pallas kernels  11.3 us (29%)
  starting transfers between devices  9.92 us (26%)
  blocking collectives  9.08 us (23%)
  waiting for transfers between devices  7.33 us (19%)
  between operations  0.75 us (2%)
    pallas_call x7, Pallas kernels, placed(): return run(*fixed)  11.3 us
    all_to_all x1, blocking collectives, body(): lax.all_to_all(message, everyone, split_axis=0, concat_axis=0, tiled=True)  9.08 us
    all_to_all x1, starting transfers between devices, body(): lax.all_to_all(message, 'wave', split_axis=0, concat_axis=0, tiled=True)  6.37 us
    all_to_all x1, waiting for transfers between devices, body(): lax.all_to_all(message, 'wave', split_axis=0, concat_axis=0, tiled=True)  4.67 us
    ppermute x3, starting transfers between devices, body(): lax.ppermute(near, 'region', [(i, i ^ s) for i in range(regions)])  3.55 us
    ppermute x3, waiting for transfers between devices, body(): lax.ppermute(near, 'region', [(i, i ^ s) for i in range(regions)])  2.67 us
  transfers between devices with their start and end apart: 4, of which 3 were waited for; matrix products, arithmetic and copies ran while one was open for 0% of the time, Pallas kernels for 17%

profile of v3, /device:TPU:0, one launch (start us, length us, event | category | flops | bytes accessed | tf_op | source)
XLA Modules:
  0.0 38.4 jit_solution(8931470327630602165)
XLA Ops:
  0.6 2.5 %shard_map.211 = f32[8,64,128]{2,1,0:T(8,128)} custom-call(f32[9,35,256]{2,1,0:T(8,128)} %q0_ref.1, f32[9,35,256]{2,1,0:T(8,128)} %q1_ref.1, f32[9,35,256]{2,1,0:T(8,128)} %q2_ref.1, s32[1,128]{1,0:T(1,128)} %bitcast.8, f32[30,32]{1,0:T(8,128)} %coarse_ref.1), custom_call_target="tpu_custom_call" | custom-call | flops 268435456 | bytes 2097152 | tf_op jit(solution)/shard_map/pallas_call | solution.py:580
  3.2 6.4 %all-to-all-start = ((f32[8,64,128]{2,1,0:T(8,128)}), f32[8,64,128]{2,1,0:T(8,128)S(1)}, u32[]{:S(2)}, u32[]{:S(2)}) async-start(f32[8,64,128]{2,1,0:T(8,128)} %shard_map.211), calls=%async_computation | async-start | bytes 524288 | tf_op jit(solution)/shard_map/all_to_all | solution.py:638
  9.5 0.0 copy-start.2
  9.6 5.0 %shard_map.213 = (f32[432,1024]{1,0:T(8,128)S(1)}, f32[9,35,256]{2,1,0:T(8,128)S(1)}, f32[9,35,256]{2,1,0:T(8,128)}, f32[9,35,256]{2,1,0:T(8,128)}, bf16[40,192]...) custom-call(f32[9,35,256]{2,1,0:T(8,128)} %q0_ref.1, ...), custom_call_target="tpu_custom_call" | custom-call | flops 4294967296 | bytes 8388608 | tf_op jit(solution)/shard_map/pallas_call | solution.py:580
  14.6 4.7 %all-to-all-done.got_ref = f32[8,64,128]{2,1,0:T(8,128)S(1)} async-done(((f32[8,64,128]{2,1,0:T(8,128)}), f32[8,64,128]{2,1,0:T(8,128)S(1)}, u32[]{:S(2)}, u32[]{:S(2)}) %all-to-all-start) | async-done | bytes 262176 | tf_op jit(solution)/shard_map/all_to_all | solution.py:638
  19.3 0.1 shard_map.212.refs_0_
  19.4 1.6 %collective-permute-start = (f32[32,256]{1,0:T(8,128)S(1)}, f32[32,256]{1,0:T(8,128)S(1)}, u32[]{:S(2)}, u32[]{:S(2)}) collective-permute-start(f32[32,256]{1,0:T(8,128)S(1)} %shard_map.212.refs_0_), channel_id=1, source_target_pairs={{0,8},{8,0},{16,24},{24,16},{1,9},{9,1},{17,25},{25,17},{2,10},{10... | collective-permute-start | bytes 98312 | tf_op jit(solution)/shard_map/ppermute | solution.py:692
  20.9 1.5 %collective-permute-start.1 = (f32[32,256]{1,0:T(8,128)S(1)}, f32[32,256]{1,0:T(8,128)S(1)}, u32[]{:S(2)}, u32[]{:S(2)}) collective-permute-start(f32[32,256]{1,0:T(8,128)S(1)} %shard_map.212.refs_0_), channel_id=1, source_target_pairs={{0,16},{8,24},{16,0},{24,8},{1,17},{9,25},{17,1},{25,9},{2,18},{10... | collective-permute-start | bytes 98312 | tf_op jit(solution)/shard_map/ppermute | solution.py:692
  22.4 0.5 %collective-permute-start.2 = (f32[32,256]{1,0:T(8,128)S(1)}, f32[32,256]{1,0:T(8,128)S(1)}, u32[]{:S(2)}, u32[]{:S(2)}) collective-permute-start(f32[32,256]{1,0:T(8,128)S(1)} %shard_map.212.refs_0_), channel_id=1, source_target_pairs={{0,24},{8,16},{16,8},{24,0},{1,25},{9,17},{17,9},{25,1},{2,26},{10... | collective-permute-start | bytes 98312 | tf_op jit(solution)/shard_map/ppermute | solution.py:692
  22.9 0.0 copy-done.2
  22.9 0.5 %shard_map.214.jump_ref = f32[432,1024]{1,0:T(8,128)S(1)} custom-call(f32[8,64,128]{2,1,0:T(8,128)S(1)} %all-to-all-done.got_ref, s32[16,1024]{1,0:T(8,128)S(1)} %get-tuple-element.26.index_ref, s32[4,256]{1,0:T(4,128)S(1)} %copy-done.2, f32[432,1024]{1,0:T(8,128)S(1)} %get-tuple-element.27.own_ref), custom_call_target="tpu_custom_call" | custom-call | flops 536870912 | bytes 2097152 | tf_op jit(solution)/shard_map/pallas_call | solution.py:580
  23.4 0.0 copy-start.3
  23.4 0.0 copy-start.4
  23.4 0.0 copy-start.5
  23.4 0.0 copy-start.6
  23.4 1.1 %shard_map.215 = (f32[9,35,256]{2,1,0:T(8,128)S(1)}, f32[9,35,256]{2,1,0:T(8,128)S(1)}, f32[9,35,256]{2,1,0:T(8,128)S(1)}) custom-call(f32[432,1024]{1,0:T(8,128)S(1)} %shard_map.214.jump_ref, bf16[40,192]{1,0:T(8,128)(2,1)S(1)} %get-tuple-element.28.lift_ref, f32[3,4,256]{2,1,0:T(4,128)S(1)} %get-tuple-element.29.normal_ref, ...), custom_call_target="tpu_custom_call" | custom-call | flops 1073741824 | bytes 4194304 | tf_op jit(solution)/shard_map/pallas_call | solution.py:580
  24.6 0.0 collective-permute-done.refs_1_
  24.6 0.2 collective-permute-done.1.refs_2_
  24.8 2.4 %collective-permute-done.2.refs_3_ = f32[32,256]{1,0:T(8,128)S(1)} collective-permute-done((f32[32,256]{1,0:T(8,128)S(1)}, f32[32,256]{1,0:T(8,128)S(1)}, u32[]{:S(2)}, u32[]{:S(2)}) %collective-permute-start.2) | collective-permute-done | bytes 32800 | tf_op jit(solution)/shard_map/ppermute | solution.py:692
  27.2 0.0 copy-done.3
  27.3 0.0 copy-done.4
  27.3 0.0 copy-done.5
  27.3 0.0 copy-done.6
  27.3 0.0 copy-start
  27.3 0.0 copy-start.1
  27.3 1.1 %shard_map.216 = (f32[9,35,256]{2,1,0:T(8,128)S(1)}, f32[9,35,256]{2,1,0:T(8,128)S(1)}, f32[32,4,128]{2,1,0:T(4,128)S(1)}) custom-call(f32[32,256]{1,0:T(8,128)S(1)} %shard_map.212.refs_0_, f32[32,256]{1,0:T(8,128)S(1)} %collective-permute-done.refs_1_, f32[32,256]{1,0:T(8,128)S(1)} %collective-permute-done.1.refs_2_, ...), custom_call_target="tpu_custom_call" | custom-call | flops 1073741824 | bytes 4194304 | tf_op jit(solution)/shard_map/pallas_call | solution.py:580
  28.4 9.1 %all_to_all.10.arrived_ref = f32[32,4,128]{2,1,0:T(4,128)S(1)} all-to-all(f32[32,4,128]{2,1,0:T(4,128)S(1)} %get-tuple-element.43), channel_id=1, replica_groups=mesh['region'=4,'wave'=8] {'region','wave'}, dimensions={0} | all-to-all | bytes 131072 | tf_op jit(solution)/shard_map/all_to_all | solution.py:712
  37.5 0.0 copy-done
  37.5 0.0 copy-done.1
  37.5 0.9 %shard_map.217 = (f32[30,32]{1,0:T(8,128)}, f32[9,35,256]{2,1,0:T(8,128)}, f32[9,35,256]{2,1,0:T(8,128)}) custom-call(f32[32,4,128]{2,1,0:T(4,128)S(1)} %all_to_all.10.arrived_ref, f32[30,32]{1,0:T(8,128)S(1)} %copy-done.1, f32[30,32]{1,0:T(8,128)S(1)} %copy-done, f32[9,35,256]{2,1,0:T(8,128)S(1)} %get-tuple-element.44.delta_ref, ...), custom_call_target="tpu_custom_call" | custom-call | tf_op jit(solution)/shard_map/pallas_call | solution.py:580
Async XLA Ops:
  3.2 16.1 %all-to-all-start = ((f32[8,64,128]{2,1,0:T(8,128)}), f32[8,64,128]{2,1,0:T(8,128)S(1)}, u32[]{:S(2)}, u32[]{:S(2)}) async-start(f32[8,64,128]{2,1,0:T(8,128)} %shard_map.211), calls=%async_computation | async-start | bytes 524288 | tf_op jit(solution)/shard_map/all_to_all | solution.py:638
  9.5 13.4 %copy-start.2 = (s32[4,256]{1,0:T(4,128)S(1)}, s32[4,256]{1,0:T(4,128)}, u32[]{:S(2)}) copy-start(s32[4,256]{1,0:T(4,128)} %neighbor_ref.3) | copy-start | bytes 12292
  19.4 5.2 %collective-permute-start = (f32[32,256]{1,0:T(8,128)S(1)}, f32[32,256]{1,0:T(8,128)S(1)}, u32[]{:S(2)}, u32[]{:S(2)}) collective-permute-start(f32[32,256]{1,0:T(8,128)S(1)} %shard_map.212.refs_0_), channel_id=1, source_target_pairs={{0,8},{8,0},{16,24},{24,16},{1,9},{9,1},{17,25},{25,17},{2,10},{10... | collective-permute-start | bytes 98312 | tf_op jit(solution)/shard_map/ppermute | solution.py:692
  20.9 3.9 %collective-permute-start.1 = (f32[32,256]{1,0:T(8,128)S(1)}, f32[32,256]{1,0:T(8,128)S(1)}, u32[]{:S(2)}, u32[]{:S(2)}) collective-permute-start(f32[32,256]{1,0:T(8,128)S(1)} %shard_map.212.refs_0_), channel_id=1, source_target_pairs={{0,16},{8,24},{16,0},{24,8},{1,17},{9,25},{17,1},{25,9},{2,18},{10... | collective-permute-start | bytes 98312 | tf_op jit(solution)/shard_map/ppermute | solution.py:692
  22.4 4.8 %collective-permute-start.2 = (f32[32,256]{1,0:T(8,128)S(1)}, f32[32,256]{1,0:T(8,128)S(1)}, u32[]{:S(2)}, u32[]{:S(2)}) collective-permute-start(f32[32,256]{1,0:T(8,128)S(1)} %shard_map.212.refs_0_), channel_id=1, source_target_pairs={{0,24},{8,16},{16,8},{24,0},{1,25},{9,17},{17,9},{25,1},{2,26},{10... | collective-permute-start | bytes 98312 | tf_op jit(solution)/shard_map/ppermute | solution.py:692
  23.4 3.9 %copy-start.3 = (f32[35,256]{1,0:T(8,128)S(1)}, f32[35,256]{1,0:T(8,128)}, u32[]{:S(2)}) copy-start(f32[35,256]{1,0:T(8,128)} %refs_13_.1) | copy-start | bytes 107524
  23.4 3.9 %copy-start.4 = (s32[256]{0:T(256)S(1)}, s32[256]{0:T(256)}, u32[]{:S(2)}) copy-start(s32[256]{0:T(256)} %param.34) | copy-start | bytes 3076
  23.4 3.8 %copy-start.5 = (f32[9,35,256]{2,1,0:T(8,128)S(1)}, f32[9,35,256]{2,1,0:T(8,128)}, u32[]{:S(2)}) copy-start(f32[9,35,256]{2,1,0:T(8,128)} %get-tuple-element.41.refs_14_) | copy-start | bytes 967684
  23.4 3.8 %copy-start.6 = (f32[9,35,256]{2,1,0:T(8,128)S(1)}, f32[9,35,256]{2,1,0:T(8,128)}, u32[]{:S(2)}) copy-start(f32[9,35,256]{2,1,0:T(8,128)} %get-tuple-element.42.refs_15_) | copy-start | bytes 967684
  27.3 10.2 %copy-start = (f32[30,32]{1,0:T(8,128)S(1)}, f32[30,32]{1,0:T(8,128)}, u32[]{:S(2)}) copy-start(f32[30,32]{1,0:T(8,128)} %coarse_ref.1) | copy-start | bytes 11524
  27.3 10.2 %copy-start.1 = (f32[30,32]{1,0:T(8,128)S(1)}, f32[30,32]{1,0:T(8,128)}, u32[]{:S(2)}) copy-start(f32[30,32]{1,0:T(8,128)} %reg_ref.1) | copy-start | bytes 11524
